TPU v7x, 32 devices: a whole 2x2x4 slice. The times are simulated.
32 devices in a mesh: stream: 2 (over y), pairs: 16 (over z, x, core).
Axes of the slice: x: 2, y: 2, z: 4, core: 2. Of those that a mesh axis runs over, the one named last changes fastest.
Arguments:
- tokens: bfloat16 [2, 2, 8192, 768], P('stream', None, 'pairs'), may hold values from -6 to 6
- segments: int32 [2, 2, 16, 512], P('stream', None, 'pairs'), may hold values from 0 to 3, never falling along the last dimension, each value on 1 to 384 neighbouring positions
- counts: int32 [2, 16], replicated, may hold values from 2 to 4
- cotangent: bfloat16 [2, 2, 8192, 768], P('stream', None, 'pairs'), may hold values from -6 to 6
- w_query: bfloat16 [768, 768], replicated, may hold values from -0.21875 to 0.21875
- b_query: bfloat16 [768], replicated, may hold values from -3 to 3
- w_key: bfloat16 [768, 768], replicated, may hold values from -0.21875 to 0.21875
- w_value: bfloat16 [768, 768], replicated, may hold values from -0.21875 to 0.21875
- b_value: bfloat16 [768], replicated, may hold values from -3 to 3
- w_out: bfloat16 [768, 768], replicated, may hold values from -0.875 to 0.875
- b_out: bfloat16 [768], replicated, may hold values from -2 to 2
- gain_attn: bfloat16 [768], replicated, may hold values from 0.5 to 1.5
- bias_attn: bfloat16 [768], replicated, may hold values from -1.5 to 1.5
- w_inner: bfloat16 [768, 3072], replicated, may hold values from -0.21875 to 0.21875
- b_inner: bfloat16 [3072], replicated, may hold values from -3 to 3
- w_outer: bfloat16 [3072, 768], replicated, may hold values from -0.109375 to 0.109375
- b_outer: bfloat16 [768], replicated, may hold values from -2 to 2
- gain_ffn: bfloat16 [768], replicated, may hold values from 0.5 to 1.5
- bias_ffn: bfloat16 [768], replicated, may hold values from -0.796875 to 0.796875
Outputs:
- loss_rows: float32 [2, 2, 64], P('stream', None, 'pairs')
- embeddings: float32 [2, 2, 64, 768], P('stream', None, 'pairs')
- embedding_grads: float32 [2, 2, 64, 768], P('stream', None, 'pairs')
- hidden_states: bfloat16 [2, 2, 8192, 768], P('stream', None, 'pairs')
- token_grads: bfloat16 [2, 2, 8192, 768], P('stream', None, 'pairs')
- grad_w_query: float32 [768, 768], replicated
- grad_b_query: float32 [768], replicated
- grad_w_key: float32 [768, 768], replicated
- grad_w_value: float32 [768, 768], replicated
- grad_b_value: float32 [768], replicated
- grad_w_out: float32 [768, 768], replicated
- grad_b_out: float32 [768], replicated
- grad_gain_attn: float32 [768], replicated
- grad_bias_attn: float32 [768], replicated
- grad_w_inner: float32 [768, 3072], replicated
- grad_b_inner: float32 [3072], replicated
- grad_w_outer: float32 [3072, 768], replicated
- grad_b_outer: float32 [768], replicated
- grad_gain_ffn: float32 [768], replicated
- grad_bias_ffn: float32 [768], replicated
All inputs are finite; a program needn't handle non-finite values.
Results may differ from a plain program's by a relative error of at most 0.014.
Values sent between devices are 32-bit elements; how exact they have to be, the bound alone decides.
No kernel may reach another device: no remote copies, remote signals or barrier semaphores. Data moves between devices by JAX's collectives and lax.ppermute only.
A program may use at most 256 MiB of HBM per device.

v0:
```python
import jax
import jax.numpy as jnp
from jax import lax
from jax.sharding import PartitionSpec as P

D = 768
HEADS = 12
HEAD_DIM = 64
SLOTS = 4


HIGHEST = lax.Precision.HIGHEST
LOGIT_DIVISOR = 0.01
NORM_EPS = 1e-12
UNIT_EPS = 1e-06


def swapped(value, axis, apart):
    return lax.ppermute(value, axis, [(i, i ^ 1 << apart) for i in range(lax.axis_size(axis))])


def norm_forward(total, norm_gain, layer_offset):
    centered = total - jnp.mean(total, axis=-1, keepdims=True)
    inv_std = lax.rsqrt(jnp.mean(centered * centered, axis=-1, keepdims=True) + NORM_EPS)
    normed = centered * inv_std
    return (normed, inv_std, normed * norm_gain + layer_offset)


def norm_backward(upstream, normed, inv_std, norm_gain):
    through = upstream * norm_gain
    grad_total = inv_std * (
        through
        - jnp.mean(through, axis=-1, keepdims=True)
        - normed * jnp.mean(through * normed, axis=-1, keepdims=True)
    )
    return (grad_total, jnp.sum(upstream * normed, axis=0), jnp.sum(upstream, axis=0))


def unit_scale(pooled):
    return (
        pooled
        * lax.rsqrt(jnp.mean(pooled * pooled, axis=-1, keepdims=True) + UNIT_EPS)
        * D ** (-0.5)
    )


def exact_gelu(values_in):
    return jax.nn.gelu(values_in, approximate=False)


def on_device(
    tokens,
    segments,
    counts,
    cotangent,
    w_query,
    b_query,
    w_key,
    w_value,
    b_value,
    w_out,
    b_out,
    gain_attn,
    bias_attn,
    w_inner,
    b_inner,
    w_outer,
    b_outer,
    gain_ffn,
    bias_ffn,
):
    weights_all = (
        w_query,
        b_query,
        w_key,
        w_value,
        b_value,
        w_out,
        b_out,
        gain_attn,
        bias_attn,
        w_inner,
        b_inner,
        w_outer,
        b_outer,
        gain_ffn,
        bias_ffn,
    )
    sample_count = tokens.shape[1]
    length = tokens.shape[2]
    slots = SLOTS
    scale = HEAD_DIM ** (-0.5)
    pair_index = lax.axis_index("pairs")
    rows_all = slots * lax.axis_size("pairs")
    f32 = jnp.float32
    bf16 = jnp.bfloat16
    bias_query = b_query.astype(f32)
    bias_value = b_value.astype(f32)
    output_bias = b_out.astype(f32)
    gain_one = gain_attn.astype(f32)
    shift_one = bias_attn.astype(f32)
    bias_inner = b_inner.astype(f32)
    bias_outer = b_outer.astype(f32)
    gain_two = gain_ffn.astype(f32)
    shift_two = bias_ffn.astype(f32)
    column_ids = jnp.arange(rows_all, dtype=jnp.int32)
    slot_ids = jnp.arange(slots, dtype=jnp.int32)
    totals = [jnp.zeros(weight.shape, f32) for weight in weights_all]
    loss_list, unit_list, unit_grad_list, hidden_list, input_grad_list = ([], [], [], [], [])
    for batch_number in range(sample_count):
        inputs_low = tokens[0, batch_number]
        inputs_full = inputs_low.astype(f32)
        segment = segments[0, batch_number, 0]
        query_flat = (jnp.dot(inputs_low, w_query, preferred_element_type=f32) + bias_query).astype(
            bf16
        )
        key_flat = jnp.dot(inputs_low, w_key, preferred_element_type=f32).astype(bf16)
        value_flat = (jnp.dot(inputs_low, w_value, preferred_element_type=f32) + bias_value).astype(
            bf16
        )
        queries = query_flat.reshape(length, HEADS, HEAD_DIM)
        keys = key_flat.reshape(length, HEADS, HEAD_DIM)
        values = value_flat.reshape(length, HEADS, HEAD_DIM)
        same_segment = (segment[:, None] == segment[None, :])[None]

        def masked_scores():
            raw_scores = (
                jnp.einsum("qhd,khd->hqk", queries, keys, preferred_element_type=f32) * scale
            )
            return jnp.where(same_segment, raw_scores, -1000000000.0)

        scores = masked_scores()
        row_top = jnp.max(scores, axis=-1, keepdims=True)
        exponent = jnp.exp(scores - row_top)
        normalizer_total = jnp.sum(exponent, axis=-1, keepdims=True)
        log_total = row_top + jnp.log(normalizer_total)
        probs = (exponent / normalizer_total).astype(bf16)
        mixed = (
            jnp.einsum("hqk,khd->qhd", probs, values, preferred_element_type=f32)
            .astype(bf16)
            .reshape(length, D)
        )
        attended = jnp.dot(mixed, w_out, preferred_element_type=f32) + output_bias
        normed_one, inv_one, first = norm_forward(inputs_full + attended, gain_one, shift_one)
        first_low = first.astype(bf16)
        inner = jnp.dot(first_low, w_inner, preferred_element_type=f32) + bias_inner
        gelu_values, gelu_back = jax.vjp(exact_gelu, inner)
        activated = gelu_values.astype(bf16)
        outer = jnp.dot(activated, w_outer, preferred_element_type=f32) + bias_outer
        normed_two, inv_two, hidden = norm_forward(first + outer, gain_two, shift_two)
        hidden_list.append(hidden.astype(bf16))
        one_hot = (segment[None, :] == slot_ids[:, None]).astype(f32)
        counted = jnp.sum(one_hot, axis=1, keepdims=True)
        pooled = jnp.dot(one_hot, hidden, precision=HIGHEST, preferred_element_type=f32) / counted
        unit_rows, unit_back = jax.vjp(unit_scale, pooled)
        unit_list.append(unit_rows)
        partner_rows = swapped(unit_rows, "stream", 0)
        others = lax.all_gather(partner_rows, "pairs", axis=0, tiled=True)
        count_row = counts[batch_number]
        column_valid = column_ids % slots < jnp.repeat(
            count_row, slots, total_repeat_length=rows_all
        )
        own_count = lax.dynamic_index_in_dim(count_row, pair_index, keepdims=False)
        row_valid = (slot_ids < own_count).astype(f32)
        target = column_ids[None, :] == (pair_index * slots + slot_ids)[:, None]
        cosine_scores = (
            jnp.dot(unit_rows, others.T, precision=HIGHEST, preferred_element_type=f32)
            / LOGIT_DIVISOR
        )
        masked = jnp.where(column_valid[None, :], cosine_scores, -1000000000.0)
        log_sum = jax.nn.logsumexp(masked, axis=-1)
        diagonal = jnp.sum(jnp.where(target, cosine_scores, 0.0), axis=-1)
        loss_list.append((log_sum - diagonal) * row_valid)
        grad_logits = (
            (jnp.exp(masked - log_sum[:, None]) - target.astype(f32))
            * row_valid[:, None]
            / LOGIT_DIVISOR
        )
        own_grad = jnp.dot(grad_logits, others, precision=HIGHEST, preferred_element_type=f32)
        column_gradient = jnp.dot(
            grad_logits.T, unit_rows, precision=HIGHEST, preferred_element_type=f32
        )
        summed_back = lax.psum_scatter(column_gradient, "pairs", scatter_dimension=0, tiled=True)
        returned = swapped(summed_back, "stream", 0)
        unit_grad = own_grad + returned
        unit_grad_list.append(unit_grad)
        (pooled_grad,) = unit_back(unit_grad)
        grad_hidden = cotangent[0, batch_number].astype(f32) + jnp.dot(
            one_hot.T, pooled_grad / counted, precision=HIGHEST, preferred_element_type=f32
        )
        grad_second, grad_gain_two, grad_shift_two = norm_backward(
            grad_hidden, normed_two, inv_two, gain_two
        )
        second_low = grad_second.astype(bf16)
        grad_w_outer = jnp.einsum("tf,td->fd", activated, second_low, preferred_element_type=f32)
        grad_b_outer = jnp.sum(grad_second, axis=0)
        grad_act = jnp.einsum("td,fd->tf", second_low, w_outer, preferred_element_type=f32)
        (grad_inner,) = gelu_back(grad_act)
        inner_low = grad_inner.astype(bf16)
        grad_w_inner = jnp.einsum("td,tf->df", first_low, inner_low, preferred_element_type=f32)
        grad_b_inner = jnp.sum(grad_inner, axis=0)
        grad_first = grad_second + jnp.einsum(
            "tf,df->td", inner_low, w_inner, preferred_element_type=f32
        )
        grad_sum_one, grad_gain_one, grad_shift_one = norm_backward(
            grad_first, normed_one, inv_one, gain_one
        )
        attended_low = grad_sum_one.astype(bf16)
        grad_w_out = jnp.einsum("td,te->de", mixed, attended_low, preferred_element_type=f32)
        grad_mixed = (
            jnp.einsum("te,de->td", attended_low, w_out, preferred_element_type=f32)
            .astype(bf16)
            .reshape(length, HEADS, HEAD_DIM)
        )
        grad_probs = jnp.einsum("qhd,khd->hqk", grad_mixed, values, preferred_element_type=f32)
        grad_values = jnp.einsum(
            "hqk,qhd->khd", probs, grad_mixed, preferred_element_type=f32
        ).reshape(length, D)
        soft_again = jnp.exp(masked_scores() - log_total)
        grad_scores = (
            soft_again * (grad_probs - jnp.sum(soft_again * grad_probs, axis=-1, keepdims=True))
        ).astype(bf16)
        grad_queries = (
            jnp.einsum("hqk,khd->qhd", grad_scores, keys, preferred_element_type=f32) * scale
        ).reshape(length, D)
        grad_keys = (
            jnp.einsum("hqk,qhd->khd", grad_scores, queries, preferred_element_type=f32) * scale
        ).reshape(length, D)
        query_low = grad_queries.astype(bf16)
        key_low = grad_keys.astype(bf16)
        value_low = grad_values.astype(bf16)
        grad_w_query = jnp.einsum("td,te->de", inputs_low, query_low, preferred_element_type=f32)
        grad_w_key = jnp.einsum("td,te->de", inputs_low, key_low, preferred_element_type=f32)
        grad_w_value = jnp.einsum("td,te->de", inputs_low, value_low, preferred_element_type=f32)
        grad_b_query = jnp.sum(grad_queries, axis=0)
        grad_b_value = jnp.sum(grad_values, axis=0)
        grad_b_out = jnp.sum(grad_sum_one, axis=0)
        grad_input = grad_sum_one
        grad_input = grad_input + jnp.einsum(
            "te,de->td", query_low, w_query, preferred_element_type=f32
        )
        grad_input = grad_input + jnp.einsum(
            "te,de->td", key_low, w_key, preferred_element_type=f32
        )
        grad_input = grad_input + jnp.einsum(
            "te,de->td", value_low, w_value, preferred_element_type=f32
        )
        input_grad_list.append(grad_input.astype(bf16))
        batch_grads = (
            grad_w_query,
            grad_b_query,
            grad_w_key,
            grad_w_value,
            grad_b_value,
            grad_w_out,
            grad_b_out,
            grad_gain_one,
            grad_shift_one,
            grad_w_inner,
            grad_b_inner,
            grad_w_outer,
            grad_b_outer,
            grad_gain_two,
            grad_shift_two,
        )
        totals = [running + added for running, added in zip(totals, batch_grads)]
    totals = list(lax.psum(tuple(totals), ("stream", "pairs")))
    return (
        jnp.stack(loss_list)[None],
        jnp.stack(unit_list)[None],
        jnp.stack(unit_grad_list)[None],
        jnp.stack(hidden_list)[None],
        jnp.stack(input_grad_list)[None],
        totals[0],
        totals[1],
        totals[2],
        totals[3],
        totals[4],
        totals[5],
        totals[6],
        totals[7],
        totals[8],
        totals[9],
        totals[10],
        totals[11],
        totals[12],
        totals[13],
        totals[14],
    )


def solution(mesh):
    in_specs = (
        P("stream", None, "pairs", None),
        P("stream", None, "pairs", None),
        P(),
        P("stream", None, "pairs", None),
        P(),
        P(),
        P(),
        P(),
        P(),
        P(),
        P(),
        P(),
        P(),
        P(),
        P(),
        P(),
        P(),
        P(),
        P(),
    )
    out_specs = (
        P("stream", None, "pairs"),
        P("stream", None, "pairs", None),
        P("stream", None, "pairs", None),
        P("stream", None, "pairs", None),
        P("stream", None, "pairs", None),
        P(),
        P(),
        P(),
        P(),
        P(),
        P(),
        P(),
        P(),
        P(),
        P(),
        P(),
        P(),
        P(),
        P(),
        P(),
    )
    return jax.shard_map(
        on_device, mesh=mesh, in_specs=in_specs, out_specs=out_specs, check_vma=False
    )
```

profile of v0, /device:TPU:0, one launch (start us, length us, event | category | flops | bytes accessed | tf_op | source)
XLA Modules:
  0.0 890.0 jit_solution(1401948497027483996)
XLA Ops:
  10.3 3.2 add_convert_fusion.3
  13.5 1.7 add_convert_fusion.5
  15.2 1.7 add_convert_fusion.2
  26.6 2.6 copy.104
  29.2 2.3 copy.109
  31.5 2.3 copy.105
  33.8 2.3 copy.110
  36.1 2.3 copy.106
  38.4 3.5 fusion.2
  41.9 3.7 fusion
  46.6 4.3 divide_convert_fusion.1
  55.7 2.1 fusion.3
  57.9 2.6 fusion.1
  60.5 2.0 copy-done.1
  62.5 3.4 divide_convert_fusion
  67.1 1.7 copy-done.3
  70.2 2.7 fusion.129
  73.0 34.6 %multiply_convert_fusion.3 = (bf16[512,3072]{1,0:T(8,128)(2,1)S(1)}, f32[512,3072]{1,0:T(8,128)}, bf16[512,3072]{1,0:T(8,128)(2,1)S(1)}, f32[512,3072]{1,0:T(8,128)}, f32[512,3072]{1,0:T(8,128)}) fusion(f32[3072]{0:T(1024)S(1)} %copy-done.89, f32[512,3072]{1,0:T(8,128)S(1)} %fusion.129, bf16[768,3072]{1,0:T(8,128)(2,1)S(1)} %bitcast.274, ...), kind=kOutput, calls=%fused_computation.37 | convolution fusion | flops 2625503232 | bytes 37771264 | tf_op jit(solution)/shard_map/dot_general | solution.py:146
  107.7 2.8 fusion.144
  112.5 3.0 collective-permute-start
  115.6 2.8 fusion.145
  128.3 22.6 %all-gather = f32[16,4,768]{2,1,0:T(4,128)S(1)} all-gather(f32[1,4,768]{2,1,0:T(4,128)S(1)} %bitcast.267), channel_id=1, replica_groups=mesh['stream'=2,'pairs'=16] {'pairs'}, dimensions={0}, use_global_device_ids=true | all-gather | bytes 208896 | tf_op jit(solution)/shard_map/all_gather | solution.py:158
  151.9 18.0 %all-gather.1 = f32[16,4,768]{2,1,0:T(4,128)S(1)} all-gather(f32[1,4,768]{2,1,0:T(4,128)S(1)} %bitcast.268), channel_id=1, replica_groups=mesh['stream'=2,'pairs'=16] {'pairs'}, dimensions={0}, use_global_device_ids=true | all-gather | bytes 208896 | tf_op jit(solution)/shard_map/all_gather | solution.py:158
  171.8 1.8 fusion.125
  173.6 1.8 fusion.122
  176.1 88.5 %all-reduce.10.cloned.1.call-done = (f32[64,768]{1,0:T(8,128)}, f32[64,768]{1,0:T(8,128)}) async-done(((f32[64,768]{1,0:T(8,128)}, f32[64,768]{1,0:T(8,128)}), (f32[64,768]{1,0:T(8,128)}, f32[64,768]{1,0:T(8,128)})) %all-reduce.10.cloned.1.call-update) | async-done | bytes 393232
  273.1 2.0 convert_add_fusion
  275.2 5.0 multiply_reduce_fusion.3
  280.3 2.9 fusion.134
  283.2 8.8 fusion.146
  292.0 7.2 multiply_reduce_fusion.5
  299.2 8.6 fusion.147
  307.8 8.6 fusion.137
  316.5 1.7 convolution_convert_fusion.1
  318.2 2.2 fusion.71
  320.4 5.6 fusion.19
  326.0 5.2 fusion.74
  332.6 6.3 bitcast_convert_fusion.2
  339.0 10.3 %multiply_reduce_fusion.1 = (f32[12,512]{1,0:T(8,128)S(1)}, f32[12,512,512]{1,2,0:T(8,128)}) fusion(f32[12,512,512]{1,2,0:T(8,128)} %copy-done.2, f32[12,512]{1,0:T(8,128)S(1)} %copy-done.72, pred[512,512]{0,1:T(8,128)(4,1)S(1)} %copy-done.23, bf16[512,12,64]{0,2,1:T(8,128)(2,1)S(1)} %bitcast.234, bf16[512,12,64]{0,2,1:T(8,128)(2,1)S(1)} %bitcast.226), kind=kOutput, calls=%fused_computation.6 | convolution fusion | flops 418375680 | bytes 27049984 | tf_op jit(solution)/shard_map/qhd,khd->hqk/dot_general | solution.py:215
  349.3 7.2 multiply_convert_fusion.1
  356.5 3.0 multiply_convert_fusion.5
  359.5 2.6 bitcast_convert_fusion.3
  364.4 1.7 convolution_convert_fusion
  367.5 6.3 bitcast_convert_fusion
  373.9 10.3 %multiply_reduce_fusion = (f32[12,512]{1,0:T(8,128)S(1)}, f32[12,512,512]{1,2,0:T(8,128)}) fusion(f32[12,512,512]{1,2,0:T(8,128)} %copy-done.1, f32[12,512]{1,0:T(8,128)S(1)} %copy-done.73, pred[512,512]{0,1:T(8,128)(4,1)S(1)} %copy-done.22, bf16[512,12,64]{0,2,1:T(8,128)(2,1)S(1)} %bitcast.236, bf16[512,12,64]{0,2,1:T(8,128)(2,1)S(1)} %bitcast.224), kind=kOutput, calls=%fused_computation.3 | convolution fusion | flops 418375680 | bytes 27049984 | tf_op jit(solution)/shard_map/qhd,khd->hqk/dot_general | solution.py:215
  384.2 7.1 multiply_convert_fusion
  391.3 2.9 multiply_convert_fusion.4
  394.2 2.5 bitcast_convert_fusion.1
  397.1 2.2 convolution_add_fusion.2
  401.8 7.7 convolution_add_fusion.1
  409.5 7.1 convolution_add_fusion
  418.5 2.2 add_bitcast_fusion
  420.8 2.2 add_bitcast_fusion.1
  423.0 2.2 add_bitcast_fusion.2
  427.4 2.0 compare_select_fusion
  430.0 1.7 bitcast_reduce_fusion
  447.4 42.3 %all-reduce.2 = (f32[768]{0:T(1024)}, f32[768]{0:T(1024)}, f32[768]{0:T(1024)}, f32[768]{0:T(1024)}, f32[768]{0:T(1024)}, /*index=5*/f32[3072]{0:T(1024)}, f32[768]{0:T(1024)}, f32[768]{0:T(1024)}, f32[768]{0:T(1024)}) all-reduce(f32[768]{0:T(1024)} %add.434, ...), channel_id=1, replica_groups=mesh['stream'=2,'pairs'=16] {'stream','pairs'}, use_global_device_ids=true, to_apply=%region_39.41 | all-reduce | flops 9216 | bytes 73728 | tf_op jit(solution)/shard_map/psum | solution.py:267
  491.1 2.5 maximum_bitcast_fusion
  503.0 357.0 %all-reduce.8.cloned.1.call-done = (f32[768,768]{0,1:T(8,128)}, f32[768,768]{0,1:T(8,128)}, f32[768,768]{0,1:T(8,128)}, f32[768,768]{1,0:T(8,128)}, f32[768,3072]{1,0:T(8,128)}, /*index=5*/f32[3072,768]{1,0:T(8,128)}) async-done(((f32[768,768]{0,1:T(8,128)}, f32[768,768]{0,1:T(8,128)}, f32[768,768]{0,1:T(8,128)}, f32[768,768]{1,0:T(8,128)}, f32[768,3072]{1,0:T(8,128)}, /*index=5*/f32[3072,768]{1,0:T(8,128)}), ...) | async-done | bytes 28311568 | tf_op jit(solution)/shard_map/psum | solution.py:267
  860.0 3.2 copy.120
  863.2 1.9 copy.121
  865.1 3.2 copy.122
  869.7 9.3 %copy.140 = f32[768,3072]{1,0:T(8,128)} copy(f32[768,3072]{1,0:T(8,128)} %get-tuple-element.263) | data formatting | bytes 18874368
  879.1 3.7 copy.141
  (434 shorter events, 85.0 us)
Async XLA Ops:
  7.2 46.4 %copy-start = (bf16[768,768]{1,0:T(8,128)(2,1)S(1)}, bf16[768,768]{1,0:T(8,128)(2,1)}, u32[]{:S(2)}) copy-start(bf16[768,768]{1,0:T(8,128)(2,1)} %param.34) | copy-start | bytes 3538948
  7.2 257.4 %all-reduce.10.cloned.1.call-start = ((), (), s32[]{:S(2)}) async-start(), calls=%async_computation.1 | async-start | bytes 786432
  23.1 30.5 %copy-start.104 = (f32[768]{0:T(1024)}, f32[768]{0:T(1024)S(1)}, u32[]{:S(2)}) copy-start(f32[768]{0:T(1024)S(1)} %convert_element_type.218) | copy-start | bytes 9220
  26.6 39.3 %copy-start.13 = (bf16[512,768]{0,1:T(8,128)(2,1)}, bf16[512,768]{0,1:T(8,128)(2,1)S(1)}, u32[]{:S(2)}) copy-start(bf16[512,768]{0,1:T(8,128)(2,1)S(1)} %copy.108) | copy-start | bytes 2359300
  62.4 7.6 slice-start.19
  69.7 238.1 %copy-start.79 = (f32[512]{0:T(512)}, f32[512]{0:T(512)S(1)}, u32[]{:S(2)}) copy-start(f32[512]{0:T(512)S(1)} %broadcast_multiply_fusion.9) | copy-start | bytes 6148
  70.1 237.7 %copy-start.82 = (f32[512]{0:T(512)}, f32[512]{0:T(512)S(1)}, u32[]{:S(2)}) copy-start(f32[512]{0:T(512)S(1)} %add_rsqrt_fusion.1) | copy-start | bytes 6148
  70.2 37.4 %slice-start.15 = ((s8[4718592]{0:T(1024)(128)(4,1)}), s8[4194304]{0:T(1024)(128)(4,1)S(1)}, s32[]{:S(2)}) async-start(s8[4718592]{0:T(1024)(128)(4,1)} %bitcast.269), calls=%async_computation.17 | async-start | bytes 8388608
  73.0 34.6 %copy-start.130 = (f32[512,3072]{1,0:T(8,128)}, f32[512,3072]{1,0:T(8,128)S(1)}, u32[]{:S(2)}) copy-start(f32[512,3072]{1,0:T(8,128)S(1)} %fusion.129) | copy-start | bytes 18874372
  73.0 34.7 %copy-start.103 = (f32[768]{0:T(1024)S(1)}, f32[768]{0:T(1024)}, u32[]{:S(2)}) copy-start(f32[768]{0:T(1024)} %convert_element_type.224) | copy-start | bytes 9220
  73.0 34.6 %slice-start.16 = ((s8[4718592]{0:T(1024)(128)(4,1)}), s8[524288]{0:T(1024)(128)(4,1)S(1)}, s32[]{:S(2)}) async-start(s8[4718592]{0:T(1024)(128)(4,1)} %bitcast.269), calls=%async_computation.18 | async-start | bytes 1048576
  107.6 8.0 copy-start.31
  110.5 7.9 copy-start.44
  110.9 7.5 copy-start.93
  111.9 163.2 %copy-start.78 = (f32[4,768]{1,0:T(4,128)}, f32[4,768]{1,0:T(4,128)S(1)}, u32[]{:S(2)}) copy-start(f32[4,768]{1,0:T(4,128)S(1)} %get-tuple-element.209) | copy-start | bytes 36868
  112.0 6.5 copy-start.113
  112.5 15.8 %collective-permute-start = (f32[4,768]{1,0:T(4,128)S(1)}, f32[4,768]{1,0:T(4,128)S(1)}, u32[]{:S(2)}, u32[]{:S(2)}) collective-permute-start(f32[4,768]{1,0:T(4,128)S(1)} %multiply_multiply_fusion.11), channel_id=1, source_target_pairs={{0,16},{16,0},{1,17},{17,1},{2,18},{18,2},{3,19},{19,3},{4,20},{20... | collective-permute-start | bytes 36872 | tf_op jit(solution)/shard_map/ppermute | solution.py:19
  118.5 8.6 copy-start.129
  119.6 55.9 %copy-start.65 = (f32[12,512]{1,0:T(8,128)S(1)}, f32[12,512]{1,0:T(8,128)}, u32[]{:S(2)}) copy-start(f32[12,512]{1,0:T(8,128)} %copy-done.64) | copy-start | bytes 73732
  119.6 55.9 %copy-start.69 = (f32[12,512]{1,0:T(8,128)S(1)}, f32[12,512]{1,0:T(8,128)}, u32[]{:S(2)}) copy-start(f32[12,512]{1,0:T(8,128)} %copy-done.68) | copy-start | bytes 73732
  120.6 154.5 %copy-start.74 = (f32[4,768]{1,0:T(4,128)}, f32[4,768]{1,0:T(4,128)S(1)}, u32[]{:S(2)}) copy-start(f32[4,768]{1,0:T(4,128)S(1)} %get-tuple-element.215) | copy-start | bytes 36868
  121.2 30.7 %collective-permute-start.1 = (f32[4,768]{1,0:T(4,128)S(1)}, f32[4,768]{1,0:T(4,128)S(1)}, u32[]{:S(2)}, u32[]{:S(2)}) collective-permute-start(f32[4,768]{1,0:T(4,128)S(1)} %multiply_multiply_fusion.10), channel_id=1, source_target_pairs={{0,16},{16,0},{1,17},{17,1},{2,18},{18,2},{3,19},{19,3},{4,20},{20... | collective-permute-start | bytes 36872 | tf_op jit(solution)/shard_map/ppermute | solution.py:19
  125.9 44.0 %copy-start.92 = (pred[64]{0:T(512)(128)(4,1)}, pred[64]{0:T(512)(128)(4,1)S(1)}, u32[]{:S(2)}) copy-start(pred[64]{0:T(512)(128)(4,1)S(1)} %fusion.117) | copy-start | bytes 196
  151.4 115.6 %copy-start.98 = (f32[4]{0:T(128)}, f32[4]{0:T(128)S(1)}, u32[]{:S(2)}) copy-start(f32[4]{0:T(128)S(1)} %get-tuple-element.210) | copy-start | bytes 52
  170.3 96.6 %copy-start.100 = (f32[4]{0:T(128)}, f32[4]{0:T(128)S(1)}, u32[]{:S(2)}) copy-start(f32[4]{0:T(128)S(1)} %get-tuple-element.216) | copy-start | bytes 52
  171.8 92.8 %copy-start.102 = (f32[4]{0:T(128)}, f32[4]{0:T(128)S(1)}, u32[]{:S(2)}) copy-start(f32[4]{0:T(128)S(1)} %get-tuple-element.196) | copy-start | bytes 52
  171.8 95.2 %copy-start.101 = (f32[4]{0:T(128)}, f32[4]{0:T(128)S(1)}, u32[]{:S(2)}) copy-start(f32[4]{0:T(128)S(1)} %get-tuple-element.137) | copy-start | bytes 52
  175.4 684.6 %all-reduce.8.cloned.1.call-start = ((), (), s32[]{:S(2)}) async-start(), calls=%async_computation | async-start | bytes 56623104 | tf_op jit(solution)/shard_map/psum | solution.py:267
  264.6 10.5 %copy-start.45 = (f32[512,768]{1,0:T(8,128)S(1)}, f32[512,768]{1,0:T(8,128)}, u32[]{:S(2)}) copy-start(f32[512,768]{1,0:T(8,128)} %copy-done.44) | copy-start | bytes 4718596
  265.5 3.8 collective-permute-start.2
  267.7 3.7 collective-permute-start.3
  270.3 9.9 %copy-start.81 = (f32[4,768]{1,0:T(4,128)}, f32[4,768]{1,0:T(4,128)S(1)}, u32[]{:S(2)}) copy-start(f32[4,768]{1,0:T(4,128)S(1)} %get-tuple-element.219) | copy-start | bytes 36868
  272.5 7.8 copy-start.76
  275.2 8.0 slice-start.17
  283.2 24.6 %copy-start.41 = (f32[512,768]{1,0:T(8,128)}, f32[512,768]{1,0:T(8,128)S(1)}, u32[]{:S(2)}) copy-start(f32[512,768]{1,0:T(8,128)S(1)} %get-tuple-element.159) | copy-start | bytes 4718596
  283.2 8.8 copy-start.62
  283.2 8.8 copy-start.116
  292.0 7.2 copy-start.131
  307.8 8.7 copy-start.52
  332.6 16.6 %slice-start.3 = ((s8[12582912]{0:T(1024)(128)(4,1)}), s8[4194304]{0:T(1024)(128)(4,1)S(1)}, s32[]{:S(2)}) async-start(s8[12582912]{0:T(1024)(128)(4,1)} %bitcast.217), calls=%async_computation.5 | async-start | bytes 8388608
  339.0 10.3 %slice-start.4 = ((s8[12582912]{0:T(1024)(128)(4,1)}), s8[4194304]{0:T(1024)(128)(4,1)S(1)}, s32[]{:S(2)}) async-start(s8[12582912]{0:T(1024)(128)(4,1)} %bitcast.217), calls=%async_computation.6 | async-start | bytes 8388608
  339.0 10.3 %slice-start.5 = ((s8[12582912]{0:T(1024)(128)(4,1)}), s8[4194304]{0:T(1024)(128)(4,1)S(1)}, s32[]{:S(2)}) async-start(s8[12582912]{0:T(1024)(128)(4,1)} %bitcast.217), calls=%async_computation.7 | async-start | bytes 8388608
  349.3 7.2 copy-start.27
  367.5 6.4 copy-start.14
  367.5 6.4 copy-start.22
  367.5 16.7 %slice-start = ((s8[12582912]{0:T(1024)(128)(4,1)}), s8[4194304]{0:T(1024)(128)(4,1)S(1)}, s32[]{:S(2)}) async-start(s8[12582912]{0:T(1024)(128)(4,1)} %bitcast.215), calls=%async_computation.2 | async-start | bytes 8388608
  373.9 10.3 %slice-start.1 = ((s8[12582912]{0:T(1024)(128)(4,1)}), s8[4194304]{0:T(1024)(128)(4,1)S(1)}, s32[]{:S(2)}) async-start(s8[12582912]{0:T(1024)(128)(4,1)} %bitcast.215), calls=%async_computation.3 | async-start | bytes 8388608
  373.9 10.3 %slice-start.2 = ((s8[12582912]{0:T(1024)(128)(4,1)}), s8[4194304]{0:T(1024)(128)(4,1)S(1)}, s32[]{:S(2)}) async-start(s8[12582912]{0:T(1024)(128)(4,1)} %bitcast.215), calls=%async_computation.4 | async-start | bytes 8388608
  384.2 7.1 copy-start.26
  394.2 6.9 slice-start.9
  394.2 7.2 slice-start.10
  400.3 9.1 %slice-start.6 = ((s8[9437184]{0:T(1024)(128)(4,1)}), s8[4194304]{0:T(1024)(128)(4,1)S(1)}, s32[]{:S(2)}) async-start(s8[9437184]{0:T(1024)(128)(4,1)} %bitcast.219), calls=%async_computation.8 | async-start | bytes 8388608
  401.8 7.7 slice-start.7
  401.8 7.7 slice-start.8
  401.8 7.7 copy-start.32
  409.5 7.1 copy-start.39
  425.2 10.2 %copy-start.11 = (f32[12,64,512]{2,1,0:T(8,128)S(1)}, f32[12,64,512]{2,1,0:T(8,128)}, u32[]{:S(2)}) copy-start(f32[12,64,512]{2,1,0:T(8,128)} %get-tuple-element.236) | copy-start | bytes 4718596
  431.8 9.8 %copy-start.86 = (f32[768]{0:T(1024)S(1)}, f32[768]{0:T(1024)}, u32[]{:S(2)}) copy-start(f32[768]{0:T(1024)} %get-tuple-element.158) | copy-start | bytes 9220
  431.8 57.9 %copy-start.77 = (f32[4,768]{1,0:T(4,128)S(1)}, f32[4,768]{1,0:T(4,128)}, u32[]{:S(2)}) copy-start(f32[4,768]{1,0:T(4,128)} %copy-done.76) | copy-start | bytes 36868
  435.5 55.6 %copy-start.55 = (bf16[1,512,768]{2,1,0:T(8,128)(2,1)S(1)}, bf16[1,512,768]{2,1,0:T(8,128)(2,1)}, u32[]{:S(2)}) copy-start(bf16[1,512,768]{2,1,0:T(8,128)(2,1)} %get-tuple-element.171) | copy-start | bytes 2359300
  436.8 56.8 %copy-start.40 = (bf16[512,12,64]{0,2,1:T(8,128)(2,1)S(1)}, bf16[512,12,64]{0,2,1:T(8,128)(2,1)}, u32[]{:S(2)}) copy-start(bf16[512,12,64]{0,2,1:T(8,128)(2,1)} %get-tuple-element.235) | copy-start | bytes 2359300
  868.3 10.7 %slice-start.12 = ((s8[9437184]{0:T(1024)(128)(4,1)}), s8[4194304]{0:T(1024)(128)(4,1)S(1)}, s32[]{:S(2)}) async-start(s8[9437184]{0:T(1024)(128)(4,1)} %bitcast.231), calls=%async_computation.14 | async-start | bytes 8388608
  869.7 9.3 %slice-start.13 = ((s8[9437184]{0:T(1024)(128)(4,1)}), s8[4194304]{0:T(1024)(128)(4,1)S(1)}, s32[]{:S(2)}) async-start(s8[9437184]{0:T(1024)(128)(4,1)} %bitcast.231), calls=%async_computation.15 | async-start | bytes 8388608
  869.7 9.3 %slice-start.14 = ((s8[9437184]{0:T(1024)(128)(4,1)}), s8[1048576]{0:T(1024)(128)(4,1)S(1)}, s32[]{:S(2)}) async-start(s8[9437184]{0:T(1024)(128)(4,1)} %bitcast.231), calls=%async_computation.16 | async-start | bytes 2097152
  (96 other events, 280.8 us)
Sparse Core Ops, SparseCore 0:
  175.5 89.0 all-reduce.9
  425.3 434.6 all-reduce.7
where the time goes:
time: 900 us; the launch traced here: 890 us
  waiting for transfers between devices  447 us (50%)
  matrix products  204 us (23%)
  blocking collectives  82.9 us (9%)
  other arithmetic  70.3 us (8%)
  local copies, waits for them, and re-layouts  64 us (7%)
  between operations  16.7 us (2%)
    psum x1, waiting for transfers between devices, on_device(): totals = list(lax.psum(tuple(totals), ('stream', 'pairs')))  357 us
    unnamed x3, waiting for transfers between devices  88.6 us
    psum x1, blocking collectives, on_device(): totals = list(lax.psum(tuple(totals), ('stream', 'pairs')))  42.3 us
    unnamed x319, local copies, waits for them, and re-layouts  41.6 us
    all_gather x2, blocking collectives, on_device(): others = lax.all_gather(partner_rows, 'pairs', axis=0, tiled=True)  40.6 us
    dot_general x2, matrix products, on_device(): inner = jnp.dot(first_low, w_inner, preferred_element_type=f32) + bias_inner  37.3 us
    dot_general x2, matrix products, on_device(): jnp.einsum('qhd,khd->hqk', grad_mixed, values, preferred_element_type=f32)  20.5 us
  transfers between devices with their start and end apart: 6, of which 4 were waited for; matrix products, arithmetic and copies ran while one was open for 5% of the time, Pallas kernels for 0%

commit v1 on v0

v1 whole, which is shorter than its diff:
```python
import functools
import jax
import jax.numpy as jnp
import numpy as np
from jax import lax
from jax.experimental import pallas as pl
from jax.experimental.pallas import tpu as pltpu
from jax.sharding import PartitionSpec as P

D = 768
HEADS = 12
HEAD_DIM = 64
SLOTS = 4
AXES = ("stream", "pairs")
F32 = jnp.float32
BF16 = jnp.bfloat16
HIGHEST = lax.Precision.HIGHEST
LOGIT_DIVISOR = 0.01
NORM_EPS = 1e-12
UNIT_EPS = 1e-06
NEG = -1000000000.0
SCALE = HEAD_DIM**-0.5
FF_CHUNK = 512
MIB = 1 << 20

TAIL_P = 0.305
TAIL = (
    0.12163973223592059,
    0.12246682364852957,
    0.10342082369335875,
    0.12102182071723708,
    -0.03797709812500149,
    0.18571719569775694,
    -0.15298848174013205,
    0.0366992308655468,
)


def dims(lhs, rhs, contract, **kw):
    return lax.dot_general(lhs, rhs, (contract, ((), ())), preferred_element_type=F32, **kw)


def matmul(lhs, rhs):
    return dims(lhs, rhs, ((1,), (0,)))


def matmul_nt(lhs, rhs):
    return dims(lhs, rhs, ((1,), (1,)))


def matmul_tn(lhs, rhs):
    return dims(lhs, rhs, ((0,), (0,)))


def norm_forward(total):
    centered = total - jnp.mean(total, axis=-1, keepdims=True)
    inv_std = lax.rsqrt(jnp.mean(centered * centered, axis=-1, keepdims=True) + NORM_EPS)
    return centered * inv_std, inv_std


def gelu_both(x):
    tail = 1.0 / (1.0 + TAIL_P * jnp.abs(x))
    poly = jnp.full_like(x, TAIL[-1])
    for coefficient in TAIL[-2::-1]:
        poly = poly * tail + coefficient
    bell = jnp.exp(-0.5 * (x * x))
    lower = poly * tail * bell
    phi = jnp.where(x >= 0, 1.0 - lower, lower)
    return x * phi, phi + x * bell * 0.3989422804014327


def segment_mask(seg_row):
    length = seg_row.shape[1]
    rows = jnp.broadcast_to(seg_row.astype(F32), (128, length))
    columns = rows.T
    wide = jnp.concatenate([columns] * (length // 128), axis=1)
    return jnp.where(wide == jnp.broadcast_to(seg_row.astype(F32), (length, length)), 0.0, NEG)


def forward_kernel(
    tokens, seg, wq, bq, wk, wv, bv, wo, bo, g1, c1, bi, bo2, g2, c2, wi_hbm, wo2_hbm,
    q_out, k_out, v_out, mixed_out, stat_out, first_out, normed1_out, act_out, slope_out,
    normed2_out, hidden_out, pooled_out, unit_out,
    wi, wo2, mask, first_f32, acc, sem,
):
    copy_in = pltpu.make_async_copy(wi_hbm, wi, sem.at[0])
    copy_out = pltpu.make_async_copy(wo2_hbm, wo2, sem.at[1])

    @pl.when(pl.program_id(0) == 0)
    def _():
        copy_in.start()
        copy_out.start()

    x = tokens[...]
    length = x.shape[0]
    q_out[...] = (matmul(x, wq[...]) + bq[...].astype(F32)).astype(BF16)
    k_out[...] = matmul(x, wk[...]).astype(BF16)
    v_out[...] = (matmul(x, wv[...]) + bv[...].astype(F32)).astype(BF16)
    mask[...] = segment_mask(seg[...])
    low_half = lax.broadcasted_iota(jnp.int32, (length, 128), 1) < HEAD_DIM

    def head_pair(pair, carry):
        lanes = pl.ds(pl.multiple_of(pair * 128, 128), 128)
        q2 = q_out[:, lanes] * BF16(SCALE)
        k2 = k_out[:, lanes]
        v2 = v_out[:, lanes].astype(F32).T.astype(BF16)
        outs = []
        for h in range(2):
            kh = jnp.where(low_half if h == 0 else ~low_half, k2, BF16(0))
            s = matmul_nt(kh, q2) + mask[...]
            top = jnp.max(s, axis=0, keepdims=True)
            e = jnp.exp(s - top)
            total = jnp.sum(e, axis=0, keepdims=True)
            o = matmul(v2[h * HEAD_DIM : (h + 1) * HEAD_DIM], e.astype(BF16)) * (1.0 / total)
            outs.append(o)
            stat_out[pl.ds(pair * 2 + h, 1), :] = top + jnp.log(total)
        mixed_out[:, lanes] = jnp.concatenate(outs, axis=0).T.astype(BF16)
        return carry

    lax.fori_loop(0, HEADS // 2, head_pair, 0)
    total = x.astype(F32) + (matmul(mixed_out[...], wo[...]) + bo[...].astype(F32))
    normed1, inv1 = norm_forward(total)
    normed1_out[...] = normed1.astype(normed1_out.dtype)
    first = normed1 * g1[...].astype(F32) + c1[...].astype(F32)
    first_f32[...] = first
    first_out[...] = first.astype(BF16)

    @pl.when(pl.program_id(0) == 0)
    def _():
        copy_in.wait()
        copy_out.wait()

    acc[...] = jnp.zeros_like(acc)

    def ff_chunk(c, carry):
        lanes = pl.ds(pl.multiple_of(c * FF_CHUNK, FF_CHUNK), FF_CHUNK)
        inner = matmul(first_out[...], wi[:, lanes]) + bi[:, lanes].astype(F32)
        act, slope = gelu_both(inner)
        act = act.astype(BF16)
        act_out[:, lanes] = act
        slope_out[:, lanes] = slope.astype(slope_out.dtype)
        acc[...] += matmul(act, wo2[lanes, :])
        return carry

    lax.fori_loop(0, wi.shape[1] // FF_CHUNK, ff_chunk, 0)
    normed2, inv2 = norm_forward(first_f32[...] + (acc[...] + bo2[...].astype(F32)))
    normed2_out[...] = normed2.astype(normed2_out.dtype)
    hidden = normed2 * g2[...].astype(F32) + c2[...].astype(F32)
    hidden_out[...] = hidden.astype(BF16)
    slots = lax.broadcasted_iota(jnp.int32, (8, length), 0)
    one_hot = jnp.where(jnp.broadcast_to(seg[...], (8, length)) == slots, 1.0, 0.0)
    counted = jnp.maximum(jnp.sum(one_hot, axis=1, keepdims=True), 1.0)
    pooled = dims(one_hot, hidden, ((1,), (0,)), precision=HIGHEST) / counted
    pooled = pooled[:SLOTS]
    pooled_out[...] = pooled
    unit_out[...] = (
        pooled * lax.rsqrt(jnp.mean(pooled * pooled, axis=-1, keepdims=True) + UNIT_EPS) * D**-0.5
    )
    stat_out[pl.ds(HEADS, 1), :] = jnp.broadcast_to(inv1, (length, 128)).T[:1]
    stat_out[pl.ds(HEADS + 1, 1), :] = jnp.broadcast_to(inv2, (length, 128)).T[:1]


def forward(tokens, segments, w):
    batches, length, _ = tokens.shape
    ff = w["inner"].shape[1]

    def per_batch(rows, cols):
        return pl.BlockSpec((None, rows, cols), lambda b: (b, 0, 0))

    def whole(a):
        return pl.BlockSpec(a.shape, lambda b: (0,) * a.ndim, pipeline_mode=pl.Buffered(1))

    hbm = pl.BlockSpec(memory_space=pl.ANY)
    vec = lambda a: a.reshape(1, -1)
    small = [
        w["query"], vec(w["b_query"]), w["key"], w["value"], vec(w["b_value"]), w["out"],
        vec(w["b_out"]), vec(w["gain1"]), vec(w["shift1"]), vec(w["b_inner"]), vec(w["b_outer"]),
        vec(w["gain2"]), vec(w["shift2"]),
    ]
    outs = [
        (length, D, BF16), (length, D, BF16), (length, D, BF16), (length, D, BF16),
        (16, length, F32), (length, D, BF16), (length, D, BF16), (length, ff, BF16),
        (length, ff, BF16), (length, D, BF16), (length, D, BF16), (SLOTS, D, F32), (SLOTS, D, F32),
    ]
    return pl.pallas_call(
        forward_kernel,
        grid=(batches,),
        in_specs=[per_batch(length, D), per_batch(1, length)] + [whole(a) for a in small] + [hbm, hbm],
        out_specs=[per_batch(r, c) for r, c, _ in outs],
        out_shape=[jax.ShapeDtypeStruct((batches, r, c), t) for r, c, t in outs],
        scratch_shapes=[
            pltpu.VMEM((D, ff), BF16),
            pltpu.VMEM((ff, D), BF16),
            pltpu.VMEM((length, length), F32),
            pltpu.VMEM((length, D), F32),
            pltpu.VMEM((length, D), F32),
            pltpu.SemaphoreType.DMA((2,)),
        ],
        compiler_params=pltpu.CompilerParams(vmem_limit_bytes=60 * MIB),
        name="forward_layer",
    )(tokens, segments, *small, w["inner"], w["outer"])


def attention_backward_kernel(q, k, v, do, stat, seg, dq_out, dk_out, dv_out, sums_out, mask):
    length = q.shape[0]
    mask[...] = segment_mask(seg[...])
    low_half = lax.broadcasted_iota(jnp.int32, (length, 128), 1) < HEAD_DIM

    def head_pair(pair, carry):
        lanes = pl.ds(pl.multiple_of(pair * 128, 128), 128)
        q2 = q[:, lanes] * BF16(SCALE)
        k2 = k[:, lanes]
        v2 = v[:, lanes]
        do2 = do[:, lanes]
        k2t = (k2.astype(F32) * SCALE).T.astype(BF16)
        dqs, dks, dvs = [], [], []
        for h in range(2):
            half = low_half if h == 0 else ~low_half
            s = matmul_nt(jnp.where(half, k2, BF16(0)), q2) + mask[...]
            p = jnp.exp(s - stat[pl.ds(pair * 2 + h, 1), :])
            dp = matmul_nt(jnp.where(half, v2, BF16(0)), do2)
            pdp = p * dp
            delta = jnp.sum(pdp, axis=0, keepdims=True)
            ds = (pdp - p * delta).astype(BF16)
            dvs.append(matmul(p.astype(BF16), do2))
            dks.append(matmul(ds, q2))
            dqs.append(matmul(k2t[h * HEAD_DIM : (h + 1) * HEAD_DIM], ds))
        dq = jnp.concatenate(dqs, axis=0).T
        dk = jnp.where(low_half, dks[0], dks[1])
        dv = jnp.where(low_half, dvs[0], dvs[1])
        dq_out[:, lanes] = dq.astype(BF16)
        dk_out[:, lanes] = dk.astype(BF16)
        dv_out[:, lanes] = dv.astype(BF16)
        sums_out[0:1, lanes] = jnp.sum(dq, axis=0, keepdims=True)
        sums_out[1:2, lanes] = jnp.sum(dv, axis=0, keepdims=True)
        return carry

    lax.fori_loop(0, HEADS // 2, head_pair, 0)


def attention_backward(q, k, v, do, stat, segments):
    batches, length, _ = q.shape

    def per_batch(rows, cols):
        return pl.BlockSpec((None, rows, cols), lambda b: (b, 0, 0))

    wide = per_batch(length, D)
    shape = jax.ShapeDtypeStruct(q.shape, BF16)
    return pl.pallas_call(
        attention_backward_kernel,
        grid=(batches,),
        in_specs=[wide, wide, wide, wide, per_batch(16, length), per_batch(1, length)],
        out_specs=[wide, wide, wide, per_batch(8, D)],
        out_shape=[shape, shape, shape, jax.ShapeDtypeStruct((batches, 8, D), F32)],
        scratch_shapes=[pltpu.VMEM((length, length), F32)],
        compiler_params=pltpu.CompilerParams(vmem_limit_bytes=48 * MIB),
        name="attention_backward",
    )(q, k, v, do, stat, segments)


def contrast_kernel(
    place, every, own, pooled, counted, valid_row, valid_col, loss_out, grad_out, pooled_grad_out
):
    rows = every.shape[0]
    everything = every[...]
    mine = own[...]

    def batch_of(r):
        return (r >> 2) & 1

    streams_col, streams_row = valid_col[1], valid_row[1:2, :]
    ok_col, ok_row = valid_col[0], valid_row[0:1, :]
    r_col = lax.broadcasted_iota(jnp.int32, (rows, 1), 0)
    r_row = lax.broadcasted_iota(jnp.int32, (1, rows), 1)
    logits = dims(everything, everything, ((1,), (1,)), precision=HIGHEST) / LOGIT_DIVISOR
    related = (batch_of(r_col) == batch_of(r_row)) & (streams_col != streams_row) & (ok_col > 0)
    masked = jnp.where(related, logits, NEG)
    top = jnp.max(masked, axis=0, keepdims=True)
    lse_row = top + jnp.log(jnp.sum(jnp.exp(masked - top), axis=0, keepdims=True))

    o_col = lax.broadcasted_iota(jnp.int32, (8, 1), 0)
    my_stream = place[1].astype(F32)
    my_partner = place[2] * 8 + o_col
    mine_at = place[0] * 8 + o_col
    my_valid = jnp.sum(jnp.where(r_row == mine_at, ok_row, 0.0), axis=1, keepdims=True)
    own_logits = dims(mine, everything, ((1,), (1,)), precision=HIGHEST) / LOGIT_DIVISOR
    other = (batch_of(o_col) == batch_of(r_row)) & (streams_row != my_stream)
    target = jnp.where(r_row == my_partner, 1.0, 0.0)
    forward_logits = jnp.where(other & (ok_row > 0), own_logits, NEG)
    own_top = jnp.max(forward_logits, axis=1, keepdims=True)
    own_lse = own_top + jnp.log(
        jnp.sum(jnp.exp(forward_logits - own_top), axis=1, keepdims=True)
    )
    loss = (own_lse - jnp.sum(target * own_logits, axis=1, keepdims=True)) * my_valid
    loss_out[...] = jnp.broadcast_to(loss, loss_out.shape)
    forward_grad = (jnp.exp(forward_logits - own_lse) - target) * my_valid
    back_logits = jnp.where(other & (my_valid > 0), own_logits, NEG)
    back_grad = jnp.where(other, (jnp.exp(back_logits - lse_row) - target) * ok_row, 0.0)
    both = (forward_grad + back_grad) / LOGIT_DIVISOR
    grad = dims(both, everything, ((1,), (0,)), precision=HIGHEST)
    grad_out[...] = grad
    pool = pooled[...]
    inv = lax.rsqrt(jnp.mean(pool * pool, axis=-1, keepdims=True) + UNIT_EPS)
    through = grad * D**-0.5
    inner = jnp.mean(pool * through, axis=-1, keepdims=True)
    pooled_grad_out[...] = (through * inv - pool * (inner * inv * inv * inv)) / counted[...]


def contrast(place, every, own, pooled, counted, valid_row, valid_col):
    rows = every.shape[0]
    smem = pl.BlockSpec(memory_space=pltpu.SMEM)
    vmem = pl.BlockSpec(memory_space=pltpu.VMEM)
    return pl.pallas_call(
        contrast_kernel,
        in_specs=[smem] + [vmem] * 6,
        out_specs=[vmem] * 3,
        out_shape=[
            jax.ShapeDtypeStruct((8, 128), F32),
            jax.ShapeDtypeStruct((8, D), F32),
            jax.ShapeDtypeStruct((8, D), F32),
        ],
        compiler_params=pltpu.CompilerParams(vmem_limit_bytes=40 * MIB),
        name="contrast",
    )(place, every, own, pooled, counted, valid_row, valid_col)


def stages(pairs):
    bits = pairs.bit_length() - 1
    p = lax.axis_index("pairs")
    s = lax.axis_index("stream")
    core = p & 1

    def table(move):
        return [
            (a * pairs + b, move(a, b)[0] * pairs + move(a, b)[1])
            for a in range(2)
            for b in range(pairs)
        ]

    made = {
        "core": (core, table(lambda a, b: (a, b ^ 1))),
        "xy": (
            jnp.where(core == 0, (p >> 1) & 1, s),
            table(lambda a, b: (a, b ^ 2) if b % 2 == 0 else (a ^ 1, b)),
        ),
        "yx": (
            jnp.where(core == 0, s, (p >> 1) & 1),
            table(lambda a, b: (a ^ 1, b) if b % 2 == 0 else (a, b ^ 2)),
        ),
    }
    for n in range(2, bits):
        made[n] = ((p >> n) & 1, table(lambda a, b, n=n: (a, b ^ (1 << n))))
    return made


def send(value, permutation):
    return lax.ppermute(value, AXES, permutation)


def gather_all(value, steps, order):
    for name in order:
        bit, permutation = steps[name]
        got = send(value, permutation)
        value = jnp.concatenate(
            [jnp.where(bit == 0, value, got), jnp.where(bit == 0, got, value)], axis=0
        )
    return value


def gather_layout(pairs, order):
    blocks = []
    for block in range(2 * pairs):
        bit = {name: (block >> at) & 1 for at, name in enumerate(order)}
        core = bit["core"]
        x, s = (bit["xy"], bit["yx"]) if core == 0 else (bit["yx"], bit["xy"])
        pair = core + 2 * x
        for name in order:
            if isinstance(name, int):
                pair += bit[name] << name
        blocks.append((s, pair))
    return np.array(blocks)


def sum_of(terms):
    total = terms[0]
    for term in terms[1:]:
        total = total + term
    return total


def half_of(terms, which):
    rows = terms[0].shape[0] // 2
    return [lax.dynamic_slice_in_dim(term, which * rows, rows, 0) for term in terms]


def grouped(jobs):
    groups = {}
    for at, (_, name) in enumerate(jobs):
        groups.setdefault(name, []).append(at)
    return groups.items()


def transfer(buffers, permutation):
    if len(buffers) == 1:
        return [send(buffers[0], permutation)]
    got = send(jnp.concatenate(buffers, axis=0), permutation)
    parts, start = [], 0
    for buffer in buffers:
        parts.append(got[start : start + buffer.shape[0]])
        start += buffer.shape[0]
    return parts


def scatter_step(steps, jobs, extra=None):
    done = [None] * len(jobs)
    for name, members in grouped(jobs):
        bit, permutation = steps[name]
        buffers = [sum_of(half_of(jobs[at][0], 1 - bit)) for at in members]
        riding = extra is not None and 0 in members
        got = transfer(buffers + ([extra] if riding else []), permutation)
        for at, part in zip(members, got):
            done[at] = [sum_of(half_of(jobs[at][0], bit)), part]
        if riding:
            summed = extra + got[-1]
    return (done, summed) if extra is not None else done


def swap_step(steps, values, name):
    got = transfer(values, steps[name][1])
    return [value + part for value, part in zip(values, got)]


def collect_step(steps, jobs):
    done = [None] * len(jobs)
    for name, members in grouped(jobs):
        bit, permutation = steps[name]
        buffers = [jobs[at][0] for at in members]
        for at, buffer, part in zip(members, buffers, transfer(buffers, permutation)):
            done[at] = jnp.concatenate(
                [jnp.where(bit == 0, buffer, part), jnp.where(bit == 0, part, buffer)], axis=0
            )
    return done


def sum_over_devices(grad, pairs, steps, extra=None):
    bits = pairs.bit_length() - 1
    tail = list(range(3, bits - 1))
    last = bits - 1
    wide_order = ["core", "xy", "yx", 2] + tail
    deep_order = ["core", 2, "yx", "xy"] + tail
    cut = grad.shape[0] * 2 // 3
    wide, deep = [grad[:cut]], [grad[cut:]]
    for a, b in zip(wide_order, deep_order):
        jobs = [(wide, a), (deep, b)]
        if extra is None:
            wide, deep = scatter_step(steps, jobs)
        else:
            (wide, deep), extra = scatter_step(steps, jobs, extra)
    values = [sum_of(wide), sum_of(deep)] + ([] if extra is None else [extra])
    values = swap_step(steps, values, last)
    wide, deep = values[:2]
    for a, b in zip(wide_order[::-1], deep_order[::-1]):
        wide, deep = collect_step(steps, [(wide, a), (deep, b)])
    total = jnp.concatenate([wide, deep], axis=0)
    return total if extra is None else (total, values[2])


def on_device(
    tokens, segments, counts, cotangent, w_query, b_query, w_key, w_value, b_value, w_out, b_out,
    gain_attn, bias_attn, w_inner, b_inner, w_outer, b_outer, gain_ffn, bias_ffn,
):
    pairs = lax.axis_size("pairs")
    bits = pairs.bit_length() - 1
    batches, length = tokens.shape[1], tokens.shape[2]
    ff = w_inner.shape[1]
    stream = lax.axis_index("stream")
    pair = lax.axis_index("pairs")
    steps = stages(pairs)
    w = dict(
        query=w_query, b_query=b_query, key=w_key, value=w_value, b_value=b_value, out=w_out,
        b_out=b_out, gain1=gain_attn, shift1=bias_attn, inner=w_inner, b_inner=b_inner,
        outer=w_outer, b_outer=b_outer, gain2=gain_ffn, shift2=bias_ffn,
    )
    x = tokens[0]
    seg = segments[0]
    order = list(range(bits - 1, 1, -1)) + ["xy", "yx", "core"]
    layout = gather_layout(pairs, order)
    slot = jnp.arange(SLOTS, dtype=jnp.int32)
    block_counts = counts[:, layout[:, 1]].T
    valid = (slot[None, None, :] < block_counts[:, :, None]).astype(F32).reshape(-1)
    streams = jnp.asarray(np.repeat(layout[:, 0], batches * SLOTS), F32)
    valid_row = jnp.stack([valid, streams])
    valid_col = valid_row[:, :, None]
    block_of = np.zeros((2, pairs), np.int32)
    for block, (s, p) in enumerate(layout):
        block_of[s, p] = block
    own_block = jnp.asarray(block_of)[stream, pair]
    partner_block = jnp.asarray(block_of)[1 - stream, pair]
    place = jnp.stack([own_block, stream, partner_block]).astype(jnp.int32)
    one_hot = (seg[:, 0, None, :] == slot[None, :, None]).astype(F32)
    counted = jnp.sum(one_hot, axis=2).reshape(batches * SLOTS, 1)

    (q, k, v, mixed, stat, first_low, normed1, act, slope, normed2, hidden, pooled, unit) = forward(
        x, seg, w
    )
    unit = unit.reshape(batches * SLOTS, D)
    every = gather_all(unit, steps, order)
    loss, unit_grad, pooled_grad = contrast(
        place, every, unit, pooled.reshape(batches * SLOTS, D), counted, valid_row, valid_col
    )
    loss = loss[:, 0].reshape(1, batches, SLOTS)

    tokens_all = batches * length
    flat = lambda a: a.reshape(tokens_all, a.shape[-1])
    inv1 = stat[:, HEADS].reshape(tokens_all, 1)
    inv2 = stat[:, HEADS + 1].reshape(tokens_all, 1)

    def norm_backward(upstream, normed, inv_std, gain):
        normed = normed.astype(F32)
        through = upstream * gain
        grad = inv_std * (
            through
            - jnp.mean(through, axis=-1, keepdims=True)
            - normed * jnp.mean(through * normed, axis=-1, keepdims=True)
        )
        return grad, jnp.sum(upstream * normed, axis=0), jnp.sum(upstream, axis=0)

    spread = jnp.zeros((batches, length, D), F32)
    pooled_grad = pooled_grad.reshape(batches, SLOTS, D)
    for number in range(SLOTS):
        spread = jnp.where(
            (seg[:, 0] == number)[:, :, None], pooled_grad[:, number][:, None, :], spread
        )
    grad_hidden = flat(cotangent[0].astype(F32) + spread)
    grad_h2, grad_gain2, grad_shift2 = norm_backward(
        grad_hidden, flat(normed2), inv2, gain_ffn.astype(F32)
    )
    d2 = grad_h2.astype(BF16)
    grad_w_outer = matmul_tn(flat(act), d2)
    grad_b_outer = jnp.sum(grad_h2, axis=0)
    grad_inner = matmul_nt(d2, w_outer) * flat(slope).astype(F32)
    d1 = grad_inner.astype(BF16)
    grad_w_inner = matmul_tn(flat(first_low), d1)
    grad_b_inner = jnp.sum(grad_inner, axis=0)
    grad_first = grad_h2 + matmul_nt(d1, w_inner)
    grad_h1, grad_gain1, grad_shift1 = norm_backward(
        grad_first, flat(normed1), inv1, gain_attn.astype(F32)
    )
    d0 = grad_h1.astype(BF16)
    grad_w_out = matmul_tn(flat(mixed), d0)
    grad_b_out = jnp.sum(grad_h1, axis=0)
    grad_mixed = matmul_nt(d0, w_out).astype(BF16).reshape(batches, length, D)
    dq, dk, dv, sums = attention_backward(q, k, v, grad_mixed, stat, seg)
    xf = flat(x)
    grad_w_query = matmul_tn(xf, flat(dq))
    grad_w_key = matmul_tn(xf, flat(dk))
    grad_w_value = matmul_tn(xf, flat(dv))
    sums = jnp.sum(sums, axis=0)
    token_grads = (
        grad_h1
        + matmul_nt(flat(dq), w_query)
        + matmul_nt(flat(dk), w_key)
        + matmul_nt(flat(dv), w_value)
    ).astype(BF16).reshape(1, batches, length, D)

    vectors = jnp.concatenate(
        [
            sums[0], sums[1], grad_b_out, grad_gain1, grad_shift1, grad_b_outer, grad_gain2,
            grad_shift2, grad_b_inner, jnp.zeros((4 * D,), F32),
        ]
    ).reshape(-1, D)
    total_outer = sum_over_devices(grad_w_outer, pairs, steps)
    total_inner = sum_over_devices(grad_w_inner, pairs, steps)
    total_attn, vectors = sum_over_devices(
        jnp.concatenate([grad_w_query, grad_w_key, grad_w_value, grad_w_out], axis=0),
        pairs, steps, vectors,
    )
    g_query, g_key, g_value, g_out = (total_attn[n * D : (n + 1) * D] for n in range(4))
    return (
        loss,
        unit.reshape(1, batches, SLOTS, D),
        unit_grad.reshape(1, batches, SLOTS, D),
        hidden[None],
        token_grads,
        g_query,
        vectors[0],
        g_key,
        g_value,
        vectors[1],
        g_out,
        vectors[2],
        vectors[3],
        vectors[4],
        total_inner,
        vectors[8 : 8 + ff // D].reshape(ff),
        total_outer,
        vectors[5],
        vectors[6],
        vectors[7],
    )


def solution(mesh):
    row = P("stream", None, "pairs", None)
    in_specs = (row, row, P(), row) + (P(),) * 15
    out_specs = (P("stream", None, "pairs"), row, row, row, row) + (P(),) * 15
    return jax.shard_map(
        on_device, mesh=mesh, in_specs=in_specs, out_specs=out_specs, check_vma=False
    )
```

time: 900 us -> 556 us (0.62)
  waiting for transfers between devices: 447 us -> 213 us
  matrix products: 204 us -> 45.2 us
  blocking collectives: 82.9 us -> 0 us
  Pallas kernels: 0 us -> 81.1 us
  starting transfers between devices: 5.08 us -> 55.2 us
  other arithmetic: 70.3 us -> 84.2 us
  between operations: 16.7 us -> 2.92 us
    psum x1 -> x0, waiting for transfers between devices: 357 us -> none  [on_device(): totals = list(lax.psum(tuple(totals), ('stream', 'pairs')))]
    ppermute x4 -> x44, waiting for transfers between devices: 1.41 us -> 213 us  [send(): return lax.ppermute(value, AXES, permutation)]
    dot_general x58 -> x12, matrix products: 204 us -> 45.2 us  [dims(): lax.dot_general(lhs, rhs, (contract, ((), ())), preferred_element_type=F3...]
    unnamed x3 -> x0, waiting for transfers between devices: 88.6 us -> none
    pallas_call x0 -> x3, Pallas kernels: none -> 81.1 us  [the longest x1 54.9 us: forward(): pl.pallas_call(forward_kernel, grid=(batches,), in_specs=[per_batch(lengt...]
    ppermute x4 -> x44, starting transfers between devices: 5 us -> 55.2 us  [send(): return lax.ppermute(value, AXES, permutation)]
    psum x1 -> x0, blocking collectives: 42.3 us -> none  [on_device(): totals = list(lax.psum(tuple(totals), ('stream', 'pairs')))]
    all_gather x2 -> x0, blocking collectives: 40.6 us -> none  [on_device(): others = lax.all_gather(partner_rows, 'pairs', axis=0, tiled=True)]
  transfers between devices with their start and end apart: 6 -> 44, of which waited for: 4 -> 24; matrix products, arithmetic and copies ran while one was open for 5% -> 17% of each run, Pallas kernels for 0% -> 0%
where the time goes in v1:
time: 556 us; the launch traced here: 546 us
  waiting for transfers between devices  213 us (38%)
  other arithmetic  84.2 us (15%)
  Pallas kernels  81.1 us (15%)
  local copies, waits for them, and re-layouts  64.5 us (12%)
  starting transfers between devices  55.2 us (10%)
  matrix products  45.2 us (8%)
    ppermute x44, waiting for transfers between devices, send(): return lax.ppermute(value, AXES, permutation)  213 us
    ppermute x44, starting transfers between devices, send(): return lax.ppermute(value, AXES, permutation)  55.2 us
    pallas_call x1, Pallas kernels, forward(): pl.pallas_call(forward_kernel, grid=(batches,), in_specs=[per_batch(lengt...  54.9 us
    dot_general x12, matrix products, dims(): lax.dot_general(lhs, rhs, (contract, ((), ())), preferred_element_type=F3...  45.2 us
    pallas_call x1, Pallas kernels, attention_backward(): pl.pallas_call(attention_backward_kernel, grid=(batches,), in_specs=[wide...  23.4 us
    concatenate x17, other arithmetic, transfer(): got = send(jnp.concatenate(buffers, axis=0), permutation)  20.2 us
    slice x13, local copies, waits for them, and re-layouts, transfer(): parts.append(got[start:start + buffer.shape[0]])  17.9 us
    unnamed x180, local copies, waits for them, and re-layouts  17.3 us
  transfers between devices with their start and end apart: 44, of which 24 were waited for; matrix products, arithmetic and copies ran while one was open for 17% of the time, Pallas kernels for 0%

profile of v1, /device:TPU:0, one launch (start us, length us, event | category | flops | bytes accessed | tf_op | source)
XLA Modules:
  0.0 546.1 jit_solution(10025219230389247519)
XLA Ops:
  12.1 54.9 %forward_layer.1 = (bf16[2,512,768]{2,1,0:T(8,128)(2,1)}, bf16[2,512,768]{2,1,0:T(8,128)(2,1)}, bf16[2,512,768]{2,1,0:T(8,128)(2,1)}, bf16[2,512,768]{2,1,0:T(8,...) custom-call(bf16[2,512,768]{2,1,0:T(8,128)(2,1)} %bitcast.149, ...), custom_call_target="tpu_custom_call" | custom-call | tf_op jit(solution)/shard_map/forward_layer/pallas_call | solution.py:185
  67.8 4.1 collective-permute-start
  80.1 3.3 collective-permute-done.2
  83.4 2.4 collective-permute-start.3
  86.6 2.8 collective-permute-done.3
  93.1 2.7 contrast.1
  95.9 4.0 fusion.8
  100.0 3.5 fusion.10
  103.5 9.0 %fusion = (f32[3072]{0:T(1024)S(1)}, bf16[1024,3072]{1,0:T(8,128)(2,1)S(1)}) fusion(bf16[2,512,3072]{2,1,0:T(8,128)(2,1)} %get-tuple-element.48, bf16[3072,768]{1,0:T(8,128)(2,1)} %wo2_hbm.1, f32[1024,768]{1,0:T(8,128)S(1)} %fusion.10), kind=kOutput, calls=%fused_computation.4 | convolution fusion | flops 4845204480 | bytes 20459520 | tf_op jit(solution)/shard_map/dot_general | solution.py:40
  112.5 2.7 copy-done.67
  115.2 5.2 fusion.40
  122.3 3.6 slice.294
  125.9 2.4 fusion.20
  128.3 5.4 fusion.41
  135.7 3.6 slice.307
  142.0 6.0 %fusion.5 = (f32[768]{0:T(1024)S(1)}, f32[1024]{0:T(1024)S(1)}, f32[1024]{0:T(1024)S(1)}, f32[768]{0:T(1024)S(1)}, f32[1024,768]{1,0:T(8,128)S(1)}) fusion(bf16[2,512,768]{2,1,0:T(8,128)(2,1)S(1)} %copy-done.52, f32[768]{0:T(1024)S(1)} %convert_element_type.99, f32[1024,768]{1,0:T(8,128)S(1)} %fusion.10, bf16[1024,3072]{1,0:T(8,128)(2,1)S(1)} %bitcast.170, ...), kind=kOutput, calls=%fused_computation.26 | convolution fusion | flops 4838912000 | bytes 18891776 | tf_op jit(solution)/shard_map/dot_general | solution.py:40
  149.3 2.6 convolution_convert_fusion
  151.9 23.4 %attention_backward.1 = (bf16[2,512,768]{2,1,0:T(8,128)(2,1)S(1)}, bf16[2,512,768]{2,1,0:T(8,128)(2,1)S(1)}, bf16[2,512,768]{2,1,0:T(8,128)(2,1)S(1)}, f32[2,8,768]{2,1,0:T(8,128)S(1)}) custom-call(bf16[2,512,768]{2,1,0:T(8,128)(2,1)} %get-tuple-element.50.q, bf16[2,512,768]{2,1,0:T(8,128)(2,1)} %get-tuple-element.51.k, ...), custom_call_target="tpu_custom_call" | custom-call | tf_op jit(solution)/shard_map/attention_backward/pallas_call | solution.py:249
  176.6 3.9 fusion.27
  184.4 2.9 convolution_bitcast_fusion.2
  187.6 2.7 pad_maximum_fusion.6
  193.1 2.5 pad_maximum_fusion.8
  196.3 2.1 pad_maximum_fusion.2
  198.7 2.5 copy-done.4
  201.1 2.5 pad_maximum_fusion.4
  203.7 2.1 slice.296
  205.8 2.6 dynamic-slice_add_fusion.3
  208.4 2.1 collective-permute-start.19
  216.3 2.2 slice.309
  219.9 2.1 slice.271
  227.2 5.4 collective-permute-done.20
  234.7 14.8 %collective-permute-done.33 = f32[256,768]{1,0:T(8,128)S(1)} collective-permute-done((f32[256,768]{1,0:T(8,128)S(1)}, f32[256,768]{1,0:T(8,128)S(1)}, u32[]{:S(2)}, u32[]{:S(2)}) %collective-permute-start.33) | collective-permute-done | bytes 786464 | tf_op jit(solution)/shard_map/ppermute | solution.py:357
  254.1 11.5 %collective-permute-done.7 = f32[256,768]{1,0:T(8,128)S(1)} collective-permute-done((f32[256,768]{1,0:T(8,128)S(1)}, f32[256,768]{1,0:T(8,128)S(1)}, u32[]{:S(2)}, u32[]{:S(2)}) %collective-permute-start.7) | collective-permute-done | bytes 786464 | tf_op jit(solution)/shard_map/ppermute | solution.py:357
  269.6 2.1 collective-permute-done.6
  274.0 3.5 collective-permute-start.8
  283.6 6.7 %collective-permute-done.34 = f32[384,768]{1,0:T(8,128)} collective-permute-done((f32[384,768]{1,0:T(8,128)}, f32[384,768]{1,0:T(8,128)}, u32[]{:S(2)}, u32[]{:S(2)}) %collective-permute-start.34) | collective-permute-done | bytes 1179680 | tf_op jit(solution)/shard_map/ppermute | solution.py:357
  295.8 9.8 %collective-permute-done.8 = f32[400,768]{1,0:T(8,128)} collective-permute-done((f32[400,768]{1,0:T(8,128)}, f32[400,768]{1,0:T(8,128)}, u32[]{:S(2)}, u32[]{:S(2)}) %collective-permute-start.8) | collective-permute-done | bytes 1228832 | tf_op jit(solution)/shard_map/ppermute | solution.py:357
  312.6 2.6 collective-permute-start.24
  315.8 15.9 %collective-permute-done.9 = f32[144,768]{1,0:T(8,128)S(1)} collective-permute-done((f32[144,768]{1,0:T(8,128)S(1)}, f32[144,768]{1,0:T(8,128)S(1)}, u32[]{:S(2)}, u32[]{:S(2)}) %collective-permute-start.9) | collective-permute-done | bytes 442400 | tf_op jit(solution)/shard_map/ppermute | solution.py:357
  331.9 36.9 %collective-permute-done.24 = f32[48,3072]{1,0:T(8,128)S(1)} collective-permute-done((f32[48,3072]{1,0:T(8,128)S(1)}, f32[48,3072]{1,0:T(8,128)S(1)}, u32[]{:S(2)}, u32[]{:S(2)}) %collective-permute-start.24) | collective-permute-done | bytes 589856 | tf_op jit(solution)/shard_map/ppermute | solution.py:357
  371.4 10.1 %collective-permute-done.37 = f32[192,768]{1,0:T(8,128)S(1)} collective-permute-done((f32[192,768]{1,0:T(8,128)S(1)}, f32[192,768]{1,0:T(8,128)S(1)}, u32[]{:S(2)}, u32[]{:S(2)}) %collective-permute-start.37) | collective-permute-done | bytes 589856 | tf_op jit(solution)/shard_map/ppermute | solution.py:357
  384.1 3.2 collective-permute-done.39
  387.3 6.5 %collective-permute-done.11 = f32[208,768]{1,0:T(8,128)S(1)} collective-permute-done((f32[208,768]{1,0:T(8,128)S(1)}, f32[208,768]{1,0:T(8,128)S(1)}, u32[]{:S(2)}, u32[]{:S(2)}) %collective-permute-start.11) | collective-permute-done | bytes 639008 | tf_op jit(solution)/shard_map/ppermute | solution.py:357
  395.6 6.7 %collective-permute-done.25 = f32[32,3072]{1,0:T(8,128)S(1)} collective-permute-done((f32[32,3072]{1,0:T(8,128)S(1)}, f32[32,3072]{1,0:T(8,128)S(1)}, u32[]{:S(2)}, u32[]{:S(2)}) %collective-permute-start.25) | collective-permute-done | bytes 393248 | tf_op jit(solution)/shard_map/ppermute | solution.py:357
  404.3 6.4 %collective-permute-done.38 = f32[128,768]{1,0:T(8,128)S(1)} collective-permute-done((f32[128,768]{1,0:T(8,128)S(1)}, f32[128,768]{1,0:T(8,128)S(1)}, u32[]{:S(2)}, u32[]{:S(2)}) %collective-permute-start.38) | collective-permute-done | bytes 393248 | tf_op jit(solution)/shard_map/ppermute | solution.py:357
  412.6 6.4 %collective-permute-done.12 = f32[128,768]{1,0:T(8,128)S(1)} collective-permute-done((f32[128,768]{1,0:T(8,128)S(1)}, f32[128,768]{1,0:T(8,128)S(1)}, u32[]{:S(2)}, u32[]{:S(2)}) %collective-permute-start.12) | collective-permute-done | bytes 393248 | tf_op jit(solution)/shard_map/ppermute | solution.py:357
  421.1 10.2 %collective-permute-done.40 = f32[384,768]{1,0:T(8,128)S(1)} collective-permute-done((f32[384,768]{1,0:T(8,128)S(1)}, f32[384,768]{1,0:T(8,128)S(1)}, u32[]{:S(2)}, u32[]{:S(2)}) %collective-permute-start.40) | collective-permute-done | bytes 1179680 | tf_op jit(solution)/shard_map/ppermute | solution.py:357
  434.2 22.9 %collective-permute-done.42 = f32[256,768]{1,0:T(8,128)S(1)} collective-permute-done((f32[256,768]{1,0:T(8,128)S(1)}, f32[256,768]{1,0:T(8,128)S(1)}, u32[]{:S(2)}, u32[]{:S(2)}) %collective-permute-start.42) | collective-permute-done | bytes 786464 | tf_op jit(solution)/shard_map/ppermute | solution.py:357
  457.4 2.4 collective-permute-done.41
  460.0 2.7 pad_maximum_fusion.9
  464.3 12.3 %collective-permute-done.28 = f32[128,3072]{1,0:T(8,128)S(1)} collective-permute-done((f32[128,3072]{1,0:T(8,128)S(1)}, f32[128,3072]{1,0:T(8,128)S(1)}, u32[]{:S(2)}, u32[]{:S(2)}) %collective-permute-start.28) | collective-permute-done | bytes 1572896 | tf_op jit(solution)/shard_map/ppermute | solution.py:357
  477.0 2.8 pad_maximum_fusion.7
  487.3 3.3 fusion.39
  492.1 13.4 %collective-permute-done.16 = f32[256,768]{1,0:T(8,128)} collective-permute-done((f32[256,768]{1,0:T(8,128)}, f32[256,768]{1,0:T(8,128)}, u32[]{:S(2)}, u32[]{:S(2)}) %collective-permute-start.16) | collective-permute-done | bytes 786464 | tf_op jit(solution)/shard_map/ppermute | solution.py:357
  506.8 2.3 broadcast_select_fusion.5
  509.2 3.0 pad_maximum_fusion.5
  514.3 2.7 add_convert_fusion
  519.0 2.2 slice_select_fusion.7
  521.9 2.4 slice_select_fusion.1
  526.6 2.6 slice_select_fusion.3
  529.3 4.0 pad_maximum_fusion
  533.3 3.9 pad_maximum_fusion.1
  539.6 2.3 slice_select_fusion.4
  541.9 3.8 pad_maximum_fusion.14
  (396 shorter events, 123.9 us)
Async XLA Ops:
  12.1 59.9 %copy-start.62 = (s32[2,16]{1,0:T(2,128)S(1)}, s32[2,16]{1,0:T(2,128)}, u32[]{:S(2)}) copy-start(s32[2,16]{1,0:T(2,128)} %param.25) | copy-start | bytes 388
  12.1 60.0 %copy-start.65 = (s32[32]{0:T(128)S(1)}, s32[32]{0:T(128)}, u32[]{:S(2)}) copy-start(s32[32]{0:T(128)} %constant.174) | copy-start | bytes 388
  12.1 63.7 %copy-start = (s32[1,2,1,512]{3,2,1,0:T(1,128)S(1)}, s32[1,2,1,512]{3,2,1,0:T(1,128)}, u32[]{:S(2)}) copy-start(s32[1,2,1,512]{3,2,1,0:T(1,128)} %param.24) | copy-start | bytes 12292
  67.0 22.6 %copy-start.64 = (f32[1,256]{1,0:T(1,128)S(1)}, f32[1,256]{1,0:T(1,128)}, u32[]{:S(2)}) copy-start(f32[1,256]{1,0:T(1,128)} %constant.173) | copy-start | bytes 3076
  67.0 22.6 %copy-start.60 = (bf16[768]{0:T(1024)(128)(2,1)S(1)}, bf16[768]{0:T(1024)(128)(2,1)}, u32[]{:S(2)}) copy-start(bf16[768]{0:T(1024)(128)(2,1)} %param.34) | copy-start | bytes 4612
  67.0 22.6 %copy-start.61 = (bf16[768]{0:T(1024)(128)(2,1)S(1)}, bf16[768]{0:T(1024)(128)(2,1)}, u32[]{:S(2)}) copy-start(bf16[768]{0:T(1024)(128)(2,1)} %param.40) | copy-start | bytes 4612
  67.0 22.6 %copy-start.59 = (f32[2,4,768]{2,1,0:T(4,128)S(1)}, f32[2,4,768]{2,1,0:T(4,128)}, u32[]{:S(2)}) copy-start(f32[2,4,768]{2,1,0:T(4,128)} %get-tuple-element.41) | copy-start | bytes 73732
  67.0 22.9 %copy-start.63 = (s32[2,16]{1,0:T(2,128)S(1)}, s32[2,16]{1,0:T(2,128)}, u32[]{:S(2)}) copy-start(s32[2,16]{1,0:T(2,128)} %constant.168.clone) | copy-start | bytes 388
  67.8 5.9 %collective-permute-start = (f32[8,768]{1,0:T(8,128)S(1)}, f32[8,768]{1,0:T(8,128)S(1)}, u32[]{:S(2)}, u32[]{:S(2)}) collective-permute-start(f32[8,768]{1,0:T(8,128)S(1)} %reshape.511.own), channel_id=1, source_target_pairs={{0,8},{1,9},{2,10},{3,11},{4,12},{5,13},{6,14},{7,15},{8,0},{9,1},... | collective-permute-start | bytes 73736 | tf_op jit(solution)/shard_map/ppermute | solution.py:357
  73.8 4.2 collective-permute-start.1
  78.0 5.4 collective-permute-start.2
  83.4 6.0 %collective-permute-start.3 = (f32[64,768]{1,0:T(8,128)S(1)}, f32[64,768]{1,0:T(8,128)S(1)}, u32[]{:S(2)}, u32[]{:S(2)}) collective-permute-start(f32[64,768]{1,0:T(8,128)S(1)} %pad_maximum_fusion.44), channel_id=1, source_target_pairs={{0,16},{1,3},{2,18},{3,1},{4,20},{5,7},{6,22},{7,5},{8,24},{9,11},... | collective-permute-start | bytes 589832 | tf_op jit(solution)/shard_map/ppermute | solution.py:357
  89.5 2.5 collective-permute-start.4
  180.6 15.5 %copy-start.27 = (f32[768,768]{1,0:T(8,128)}, f32[768,768]{1,0:T(8,128)S(1)}, u32[]{:S(2)}) copy-start(f32[768,768]{1,0:T(8,128)S(1)} %fusion.27) | copy-start | bytes 7077892
  182.1 14.3 %copy-start.5 = (f32[768,768]{1,0:T(8,128)}, f32[768,768]{1,0:T(8,128)S(1)}, u32[]{:S(2)}) copy-start(f32[768,768]{1,0:T(8,128)S(1)} %convolution_bitcast_fusion) | copy-start | bytes 7077892
  190.3 13.3 %collective-permute-start.18 = (f32[384,3072]{1,0:T(8,128)}, f32[384,3072]{1,0:T(8,128)}, u32[]{:S(2)}, u32[]{:S(2)}) collective-permute-start(f32[384,3072]{1,0:T(8,128)} %pad_maximum_fusion.6), channel_id=1, source_target_pairs={{0,1},{1,0},{2,3},{3,2},{4,5},{5,4},{6,7},{7,6},{8,9},{9,8},{10,11... | collective-permute-start | bytes 14155784 | tf_op jit(solution)/shard_map/ppermute | solution.py:357
  195.6 17.9 %collective-permute-start.31 = (f32[1536,768]{1,0:T(8,128)}, f32[1536,768]{1,0:T(8,128)}, u32[]{:S(2)}, u32[]{:S(2)}) collective-permute-start(f32[1536,768]{1,0:T(8,128)} %pad_maximum_fusion.8), channel_id=1, source_target_pairs={{0,1},{1,0},{2,3},{3,2},{4,5},{5,4},{6,7},{7,6},{8,9},{9,8},{10,11... | collective-permute-start | bytes 14155784 | tf_op jit(solution)/shard_map/ppermute | solution.py:357
  203.6 16.2 %collective-permute-start.5 = (f32[1552,768]{1,0:T(8,128)}, f32[1552,768]{1,0:T(8,128)}, u32[]{:S(2)}, u32[]{:S(2)}) collective-permute-start(f32[1552,768]{1,0:T(8,128)} %pad_maximum_fusion.4), channel_id=1, source_target_pairs={{0,1},{1,0},{2,3},{3,2},{4,5},{5,4},{6,7},{7,6},{8,9},{9,8},{10,11... | collective-permute-start | bytes 14303240 | tf_op jit(solution)/shard_map/ppermute | solution.py:357
  208.4 42.0 %collective-permute-start.19 = (f32[128,3072]{1,0:T(8,128)S(1)}, f32[128,3072]{1,0:T(8,128)S(1)}, u32[]{:S(2)}, u32[]{:S(2)}) collective-permute-start(f32[128,3072]{1,0:T(8,128)S(1)} %get-tuple-element.89), channel_id=1, source_target_pairs={{0,2},{1,17},{2,0},{3,19},{4,6},{5,21},{6,4},{7,23},{8,10},{9,25},... | collective-permute-start | bytes 4718600 | tf_op jit(solution)/shard_map/ppermute | solution.py:357
  212.2 20.4 %collective-permute-start.20 = (f32[64,3072]{1,0:T(8,128)S(1)}, f32[64,3072]{1,0:T(8,128)S(1)}, u32[]{:S(2)}, u32[]{:S(2)}) collective-permute-start(f32[64,3072]{1,0:T(8,128)S(1)} %get-tuple-element.109), channel_id=1, source_target_pairs={{0,4},{1,5},{2,6},{3,7},{4,0},{5,1},{6,2},{7,3},{8,12},{9,13},{10,... | collective-permute-start | bytes 2359304 | tf_op jit(solution)/shard_map/ppermute | solution.py:357
  215.5 34.0 %collective-permute-start.33 = (f32[256,768]{1,0:T(8,128)S(1)}, f32[256,768]{1,0:T(8,128)S(1)}, u32[]{:S(2)}, u32[]{:S(2)}) collective-permute-start(f32[256,768]{1,0:T(8,128)S(1)} %get-tuple-element.107), channel_id=1, source_target_pairs={{0,4},{1,5},{2,6},{3,7},{4,0},{5,1},{6,2},{7,3},{8,12},{9,13},{10,... | collective-permute-start | bytes 2359304 | tf_op jit(solution)/shard_map/ppermute | solution.py:357
  219.0 47.4 %collective-permute-start.32 = (f32[512,768]{1,0:T(8,128)S(1)}, f32[512,768]{1,0:T(8,128)S(1)}, u32[]{:S(2)}, u32[]{:S(2)}) collective-permute-start(f32[512,768]{1,0:T(8,128)S(1)} %get-tuple-element.87), channel_id=1, source_target_pairs={{0,2},{1,17},{2,0},{3,19},{4,6},{5,21},{6,4},{7,23},{8,10},{9,25},... | collective-permute-start | bytes 4718600 | tf_op jit(solution)/shard_map/ppermute | solution.py:357
  223.6 48.1 %collective-permute-start.6 = (f32[528,768]{1,0:T(8,128)S(1)}, f32[528,768]{1,0:T(8,128)S(1)}, u32[]{:S(2)}, u32[]{:S(2)}) collective-permute-start(f32[528,768]{1,0:T(8,128)S(1)} %pad_maximum_fusion.16), channel_id=1, source_target_pairs={{0,2},{1,17},{2,0},{3,19},{4,6},{5,21},{6,4},{7,23},{8,10},{9,25},... | collective-permute-start | bytes 4866056 | tf_op jit(solution)/shard_map/ppermute | solution.py:357
  232.6 33.0 %collective-permute-start.7 = (f32[256,768]{1,0:T(8,128)S(1)}, f32[256,768]{1,0:T(8,128)S(1)}, u32[]{:S(2)}, u32[]{:S(2)}) collective-permute-start(f32[256,768]{1,0:T(8,128)S(1)} %get-tuple-element.105), channel_id=1, source_target_pairs={{0,4},{1,5},{2,6},{3,7},{4,0},{5,1},{6,2},{7,3},{8,12},{9,13},{10,... | collective-permute-start | bytes 2359304 | tf_op jit(solution)/shard_map/ppermute | solution.py:357
  252.5 25.1 %collective-permute-start.21 = (f32[96,3072]{1,0:T(8,128)}, f32[96,3072]{1,0:T(8,128)}, u32[]{:S(2)}, u32[]{:S(2)}) collective-permute-start(f32[96,3072]{1,0:T(8,128)} %pad_maximum_fusion.25), channel_id=1, source_target_pairs={{0,16},{1,3},{2,18},{3,1},{4,20},{5,7},{6,22},{7,5},{8,24},{9,11},... | collective-permute-start | bytes 3538952 | tf_op jit(solution)/shard_map/ppermute | solution.py:357
  268.6 21.7 %collective-permute-start.34 = (f32[384,768]{1,0:T(8,128)}, f32[384,768]{1,0:T(8,128)}, u32[]{:S(2)}, u32[]{:S(2)}) collective-permute-start(f32[384,768]{1,0:T(8,128)} %pad_maximum_fusion.27), channel_id=1, source_target_pairs={{0,16},{1,3},{2,18},{3,1},{4,20},{5,7},{6,22},{7,5},{8,24},{9,11},... | collective-permute-start | bytes 3538952 | tf_op jit(solution)/shard_map/ppermute | solution.py:357
  274.0 31.6 %collective-permute-start.8 = (f32[400,768]{1,0:T(8,128)}, f32[400,768]{1,0:T(8,128)}, u32[]{:S(2)}, u32[]{:S(2)}) collective-permute-start(f32[400,768]{1,0:T(8,128)} %pad_maximum_fusion.23), channel_id=1, source_target_pairs={{0,16},{1,3},{2,18},{3,1},{4,20},{5,7},{6,22},{7,5},{8,24},{9,11},... | collective-permute-start | bytes 3686408 | tf_op jit(solution)/shard_map/ppermute | solution.py:357
  277.6 13.8 %copy-start.54 = (f32[128,768]{1,0:T(8,128)S(1)}, f32[128,768]{1,0:T(8,128)}, u32[]{:S(2)}) copy-start(f32[128,768]{1,0:T(8,128)} %get-tuple-element.137) | copy-start | bytes 1179652
  279.7 30.9 %collective-permute-start.23 = (f32[16,3072]{1,0:T(8,128)S(1)}, f32[16,3072]{1,0:T(8,128)S(1)}, u32[]{:S(2)}, u32[]{:S(2)}) collective-permute-start(f32[16,3072]{1,0:T(8,128)S(1)} %dynamic-slice_add_fusion.26), channel_id=1, source_target_pairs={{0,2},{1,17},{2,0},{3,19},{4,6},{5,21},{6,4},{7,23},{8,10},{9,25},... | collective-permute-start | bytes 589832 | tf_op jit(solution)/shard_map/ppermute | solution.py:357
  282.1 12.3 %copy-start.49 = (f32[256,768]{1,0:T(8,128)S(1)}, f32[256,768]{1,0:T(8,128)}, u32[]{:S(2)}) copy-start(f32[256,768]{1,0:T(8,128)} %get-tuple-element.114) | copy-start | bytes 2359300
  282.2 24.4 %copy-start.55 = (f32[128,768]{1,0:T(8,128)S(1)}, f32[128,768]{1,0:T(8,128)}, u32[]{:S(2)}) copy-start(f32[128,768]{1,0:T(8,128)} %get-tuple-element.150) | copy-start | bytes 1179652
  282.2 30.2 %collective-permute-start.22 = (f32[32,3072]{1,0:T(8,128)S(1)}, f32[32,3072]{1,0:T(8,128)S(1)}, u32[]{:S(2)}, u32[]{:S(2)}) collective-permute-start(f32[32,3072]{1,0:T(8,128)S(1)} %dynamic-slice_add_fusion.20), channel_id=1, source_target_pairs={{0,4},{1,5},{2,6},{3,7},{4,0},{5,1},{6,2},{7,3},{8,12},{9,13},{10,... | collective-permute-start | bytes 1179656 | tf_op jit(solution)/shard_map/ppermute | solution.py:357
  291.4 20.5 %collective-permute-start.36 = (f32[64,768]{1,0:T(8,128)S(1)}, f32[64,768]{1,0:T(8,128)S(1)}, u32[]{:S(2)}, u32[]{:S(2)}) collective-permute-start(f32[64,768]{1,0:T(8,128)S(1)} %dynamic-slice_add_fusion.25), channel_id=1, source_target_pairs={{0,2},{1,17},{2,0},{3,19},{4,6},{5,21},{6,4},{7,23},{8,10},{9,25},... | collective-permute-start | bytes 589832 | tf_op jit(solution)/shard_map/ppermute | solution.py:357
  294.4 16.1 %copy-start.50 = (f32[256,768]{1,0:T(8,128)S(1)}, f32[256,768]{1,0:T(8,128)}, u32[]{:S(2)}) copy-start(f32[256,768]{1,0:T(8,128)} %get-tuple-element.125) | copy-start | bytes 2359300
  294.5 20.8 %collective-permute-start.35 = (f32[128,768]{1,0:T(8,128)S(1)}, f32[128,768]{1,0:T(8,128)S(1)}, u32[]{:S(2)}, u32[]{:S(2)}) collective-permute-start(f32[128,768]{1,0:T(8,128)S(1)} %dynamic-slice_add_fusion.17), channel_id=1, source_target_pairs={{0,4},{1,5},{2,6},{3,7},{4,0},{5,1},{6,2},{7,3},{8,12},{9,13},{10,... | collective-permute-start | bytes 1179656 | tf_op jit(solution)/shard_map/ppermute | solution.py:357
  306.7 5.7 %collective-permute-start.10 = (f32[64,768]{1,0:T(8,128)S(1)}, f32[64,768]{1,0:T(8,128)S(1)}, u32[]{:S(2)}, u32[]{:S(2)}) collective-permute-start(f32[64,768]{1,0:T(8,128)S(1)} %dynamic-slice_add_fusion.27), channel_id=1, source_target_pairs={{0,2},{1,17},{2,0},{3,19},{4,6},{5,21},{6,4},{7,23},{8,10},{9,25},... | collective-permute-start | bytes 589832 | tf_op jit(solution)/shard_map/ppermute | solution.py:357
  310.6 21.1 %collective-permute-start.9 = (f32[144,768]{1,0:T(8,128)S(1)}, f32[144,768]{1,0:T(8,128)S(1)}, u32[]{:S(2)}, u32[]{:S(2)}) collective-permute-start(f32[144,768]{1,0:T(8,128)S(1)} %pad_maximum_fusion.39), channel_id=1, source_target_pairs={{0,4},{1,5},{2,6},{3,7},{4,0},{5,1},{6,2},{7,3},{8,12},{9,13},{10,... | collective-permute-start | bytes 1327112 | tf_op jit(solution)/shard_map/ppermute | solution.py:357
  312.6 56.2 %collective-permute-start.24 = (f32[48,3072]{1,0:T(8,128)S(1)}, f32[48,3072]{1,0:T(8,128)S(1)}, u32[]{:S(2)}, u32[]{:S(2)}) collective-permute-start(f32[48,3072]{1,0:T(8,128)S(1)} %pad_maximum_fusion.37), channel_id=1, source_target_pairs={{0,8},{1,9},{2,10},{3,11},{4,12},{5,13},{6,14},{7,15},{8,0},{9,1},... | collective-permute-start | bytes 1769480 | tf_op jit(solution)/shard_map/ppermute | solution.py:357
  315.4 66.2 %collective-permute-start.37 = (f32[192,768]{1,0:T(8,128)S(1)}, f32[192,768]{1,0:T(8,128)S(1)}, u32[]{:S(2)}, u32[]{:S(2)}) collective-permute-start(f32[192,768]{1,0:T(8,128)S(1)} %pad_maximum_fusion.38), channel_id=1, source_target_pairs={{0,8},{1,9},{2,10},{3,11},{4,12},{5,13},{6,14},{7,15},{8,0},{9,1},... | collective-permute-start | bytes 1769480 | tf_op jit(solution)/shard_map/ppermute | solution.py:357
  331.9 61.9 %collective-permute-start.11 = (f32[208,768]{1,0:T(8,128)S(1)}, f32[208,768]{1,0:T(8,128)S(1)}, u32[]{:S(2)}, u32[]{:S(2)}) collective-permute-start(f32[208,768]{1,0:T(8,128)S(1)} %pad_maximum_fusion.36), channel_id=1, source_target_pairs={{0,8},{1,9},{2,10},{3,11},{4,12},{5,13},{6,14},{7,15},{8,0},{9,1},... | collective-permute-start | bytes 1916936 | tf_op jit(solution)/shard_map/ppermute | solution.py:357
  368.8 15.3 %collective-permute-start.26 = (f32[16,3072]{1,0:T(8,128)S(1)}, f32[16,3072]{1,0:T(8,128)S(1)}, u32[]{:S(2)}, u32[]{:S(2)}) collective-permute-start(f32[16,3072]{1,0:T(8,128)S(1)} %slice_add_fusion.5), channel_id=1, source_target_pairs={{0,2},{1,17},{2,0},{3,19},{4,6},{5,21},{6,4},{7,23},{8,10},{9,25},... | collective-permute-start | bytes 589832 | tf_op jit(solution)/shard_map/ppermute | solution.py:357
  370.7 31.5 %collective-permute-start.25 = (f32[32,3072]{1,0:T(8,128)S(1)}, f32[32,3072]{1,0:T(8,128)S(1)}, u32[]{:S(2)}, u32[]{:S(2)}) collective-permute-start(f32[32,3072]{1,0:T(8,128)S(1)} %slice_add_fusion.1), channel_id=1, source_target_pairs={{0,4},{1,5},{2,6},{3,7},{4,0},{5,1},{6,2},{7,3},{8,12},{9,13},{10,... | collective-permute-start | bytes 1179656 | tf_op jit(solution)/shard_map/ppermute | solution.py:357
  381.6 5.7 %collective-permute-start.39 = (f32[64,768]{1,0:T(8,128)S(1)}, f32[64,768]{1,0:T(8,128)S(1)}, u32[]{:S(2)}, u32[]{:S(2)}) collective-permute-start(f32[64,768]{1,0:T(8,128)S(1)} %slice_add_fusion.4), channel_id=1, source_target_pairs={{0,2},{1,17},{2,0},{3,19},{4,6},{5,21},{6,4},{7,23},{8,10},{9,25},... | collective-permute-start | bytes 589832 | tf_op jit(solution)/shard_map/ppermute | solution.py:357
  383.4 27.2 %collective-permute-start.38 = (f32[128,768]{1,0:T(8,128)S(1)}, f32[128,768]{1,0:T(8,128)S(1)}, u32[]{:S(2)}, u32[]{:S(2)}) collective-permute-start(f32[128,768]{1,0:T(8,128)S(1)} %slice_add_fusion), channel_id=1, source_target_pairs={{0,4},{1,5},{2,6},{3,7},{4,0},{5,1},{6,2},{7,3},{8,12},{9,13},{10,... | collective-permute-start | bytes 1179656 | tf_op jit(solution)/shard_map/ppermute | solution.py:357
  393.8 18.7 %collective-permute-start.13 = (f32[64,768]{1,0:T(8,128)S(1)}, f32[64,768]{1,0:T(8,128)S(1)}, u32[]{:S(2)}, u32[]{:S(2)}) collective-permute-start(f32[64,768]{1,0:T(8,128)S(1)} %slice_add_fusion.6), channel_id=1, source_target_pairs={{0,2},{1,17},{2,0},{3,19},{4,6},{5,21},{6,4},{7,23},{8,10},{9,25},... | collective-permute-start | bytes 589832 | tf_op jit(solution)/shard_map/ppermute | solution.py:357
  402.4 18.5 %collective-permute-start.27 = (f32[96,3072]{1,0:T(8,128)S(1)}, f32[96,3072]{1,0:T(8,128)S(1)}, u32[]{:S(2)}, u32[]{:S(2)}) collective-permute-start(f32[96,3072]{1,0:T(8,128)S(1)} %pad_maximum_fusion.26), channel_id=1, source_target_pairs={{0,16},{1,3},{2,18},{3,1},{4,20},{5,7},{6,22},{7,5},{8,24},{9,11},... | collective-permute-start | bytes 3538952 | tf_op jit(solution)/shard_map/ppermute | solution.py:357
  404.2 14.8 %collective-permute-start.12 = (f32[128,768]{1,0:T(8,128)S(1)}, f32[128,768]{1,0:T(8,128)S(1)}, u32[]{:S(2)}, u32[]{:S(2)}) collective-permute-start(f32[128,768]{1,0:T(8,128)S(1)} %slice_add_fusion.2), channel_id=1, source_target_pairs={{0,4},{1,5},{2,6},{3,7},{4,0},{5,1},{6,2},{7,3},{8,12},{9,13},{10,... | collective-permute-start | bytes 1179656 | tf_op jit(solution)/shard_map/ppermute | solution.py:357
  410.8 20.5 %collective-permute-start.40 = (f32[384,768]{1,0:T(8,128)S(1)}, f32[384,768]{1,0:T(8,128)S(1)}, u32[]{:S(2)}, u32[]{:S(2)}) collective-permute-start(f32[384,768]{1,0:T(8,128)S(1)} %pad_maximum_fusion.28), channel_id=1, source_target_pairs={{0,16},{1,3},{2,18},{3,1},{4,20},{5,7},{6,22},{7,5},{8,24},{9,11},... | collective-permute-start | bytes 3538952 | tf_op jit(solution)/shard_map/ppermute | solution.py:357
  419.1 61.9 %collective-permute-start.14 = (f32[384,768]{1,0:T(8,128)S(1)}, f32[384,768]{1,0:T(8,128)S(1)}, u32[]{:S(2)}, u32[]{:S(2)}) collective-permute-start(f32[384,768]{1,0:T(8,128)S(1)} %pad_maximum_fusion.24), channel_id=1, source_target_pairs={{0,16},{1,3},{2,18},{3,1},{4,20},{5,7},{6,22},{7,5},{8,24},{9,11},... | collective-permute-start | bytes 3538952 | tf_op jit(solution)/shard_map/ppermute | solution.py:357
  421.0 36.2 %collective-permute-start.29 = (f32[64,3072]{1,0:T(8,128)S(1)}, f32[64,3072]{1,0:T(8,128)S(1)}, u32[]{:S(2)}, u32[]{:S(2)}) collective-permute-start(f32[64,3072]{1,0:T(8,128)S(1)} %pad_maximum_fusion.33), channel_id=1, source_target_pairs={{0,4},{1,5},{2,6},{3,7},{4,0},{5,1},{6,2},{7,3},{8,12},{9,13},{10,... | collective-permute-start | bytes 2359304 | tf_op jit(solution)/shard_map/ppermute | solution.py:357
  431.4 25.7 %collective-permute-start.42 = (f32[256,768]{1,0:T(8,128)S(1)}, f32[256,768]{1,0:T(8,128)S(1)}, u32[]{:S(2)}, u32[]{:S(2)}) collective-permute-start(f32[256,768]{1,0:T(8,128)S(1)} %pad_maximum_fusion.35), channel_id=1, source_target_pairs={{0,4},{1,5},{2,6},{3,7},{4,0},{5,1},{6,2},{7,3},{8,12},{9,13},{10,... | collective-permute-start | bytes 2359304 | tf_op jit(solution)/shard_map/ppermute | solution.py:357
  431.7 28.0 %collective-permute-start.41 = (f32[512,768]{1,0:T(8,128)S(1)}, f32[512,768]{1,0:T(8,128)S(1)}, u32[]{:S(2)}, u32[]{:S(2)}) collective-permute-start(f32[512,768]{1,0:T(8,128)S(1)} %pad_maximum_fusion.21), channel_id=1, source_target_pairs={{0,2},{1,17},{2,0},{3,19},{4,6},{5,21},{6,4},{7,23},{8,10},{9,25},... | collective-permute-start | bytes 4718600 | tf_op jit(solution)/shard_map/ppermute | solution.py:357
  433.7 42.9 %collective-permute-start.28 = (f32[128,3072]{1,0:T(8,128)S(1)}, f32[128,3072]{1,0:T(8,128)S(1)}, u32[]{:S(2)}, u32[]{:S(2)}) collective-permute-start(f32[128,3072]{1,0:T(8,128)S(1)} %pad_maximum_fusion.19), channel_id=1, source_target_pairs={{0,2},{1,17},{2,0},{3,19},{4,6},{5,21},{6,4},{7,23},{8,10},{9,25},... | collective-permute-start | bytes 4718600 | tf_op jit(solution)/shard_map/ppermute | solution.py:357
  457.4 19.6 %copy-start.29 = (f32[64,3072]{1,0:T(8,128)}, f32[64,3072]{1,0:T(8,128)S(1)}, u32[]{:S(2)}) copy-start(f32[64,3072]{1,0:T(8,128)S(1)} %get-tuple-element.139) | copy-start | bytes 2359300
  457.4 19.6 %copy-start.31 = (f32[64,3072]{1,0:T(8,128)}, f32[64,3072]{1,0:T(8,128)S(1)}, u32[]{:S(2)}) copy-start(f32[64,3072]{1,0:T(8,128)S(1)} %get-tuple-element.140) | copy-start | bytes 2359300
  463.1 55.9 %collective-permute-start.43 = (f32[1536,768]{1,0:T(8,128)}, f32[1536,768]{1,0:T(8,128)}, u32[]{:S(2)}, u32[]{:S(2)}) collective-permute-start(f32[1536,768]{1,0:T(8,128)} %pad_maximum_fusion.9), channel_id=1, source_target_pairs={{0,1},{1,0},{2,3},{3,2},{4,5},{5,4},{6,7},{7,6},{8,9},{9,8},{10,11... | collective-permute-start | bytes 14155784 | tf_op jit(solution)/shard_map/ppermute | solution.py:357
  480.2 44.1 %collective-permute-start.30 = (f32[384,3072]{1,0:T(8,128)}, f32[384,3072]{1,0:T(8,128)}, u32[]{:S(2)}, u32[]{:S(2)}) collective-permute-start(f32[384,3072]{1,0:T(8,128)} %pad_maximum_fusion.7), channel_id=1, source_target_pairs={{0,1},{1,0},{2,3},{3,2},{4,5},{5,4},{6,7},{7,6},{8,9},{9,8},{10,11... | collective-permute-start | bytes 14155784 | tf_op jit(solution)/shard_map/ppermute | solution.py:357
  482.5 24.3 %collective-permute-start.15 = (f32[512,768]{1,0:T(8,128)}, f32[512,768]{1,0:T(8,128)}, u32[]{:S(2)}, u32[]{:S(2)}) collective-permute-start(f32[512,768]{1,0:T(8,128)} %pad_maximum_fusion.17), channel_id=1, source_target_pairs={{0,2},{1,17},{2,0},{3,19},{4,6},{5,21},{6,4},{7,23},{8,10},{9,25},... | collective-permute-start | bytes 4718600 | tf_op jit(solution)/shard_map/ppermute | solution.py:357
  486.0 19.5 %collective-permute-start.16 = (f32[256,768]{1,0:T(8,128)}, f32[256,768]{1,0:T(8,128)}, u32[]{:S(2)}, u32[]{:S(2)}) collective-permute-start(f32[256,768]{1,0:T(8,128)} %pad_maximum_fusion.31), channel_id=1, source_target_pairs={{0,4},{1,5},{2,6},{3,7},{4,0},{5,1},{6,2},{7,3},{8,12},{9,13},{10,... | collective-permute-start | bytes 2359304 | tf_op jit(solution)/shard_map/ppermute | solution.py:357
  490.6 14.8 %copy-start.45 = (f32[128,768]{1,0:T(8,128)S(1)}, f32[128,768]{1,0:T(8,128)}, u32[]{:S(2)}) copy-start(f32[128,768]{1,0:T(8,128)} %copy-done.44) | copy-start | bytes 1179652
  490.6 14.8 %copy-start.47 = (f32[128,768]{1,0:T(8,128)S(1)}, f32[128,768]{1,0:T(8,128)}, u32[]{:S(2)}) copy-start(f32[128,768]{1,0:T(8,128)} %copy-done.46) | copy-start | bytes 1179652
  492.1 14.8 %copy-start.40 = (f32[256,768]{1,0:T(8,128)S(1)}, f32[256,768]{1,0:T(8,128)}, u32[]{:S(2)}) copy-start(f32[256,768]{1,0:T(8,128)} %copy-done.39) | copy-start | bytes 2359300
  492.1 14.8 %copy-start.42 = (f32[256,768]{1,0:T(8,128)S(1)}, f32[256,768]{1,0:T(8,128)}, u32[]{:S(2)}) copy-start(f32[256,768]{1,0:T(8,128)} %copy-done.41) | copy-start | bytes 2359300
  513.2 24.1 %collective-permute-start.17 = (f32[1536,768]{1,0:T(8,128)}, f32[1536,768]{1,0:T(8,128)}, u32[]{:S(2)}, u32[]{:S(2)}) collective-permute-start(f32[1536,768]{1,0:T(8,128)} %pad_maximum_fusion.5), channel_id=1, source_target_pairs={{0,1},{1,0},{2,3},{3,2},{4,5},{5,4},{6,7},{7,6},{8,9},{9,8},{10,11... | collective-permute-start | bytes 14155784 | tf_op jit(solution)/shard_map/ppermute | solution.py:357
  (62 other events, 237.7 us)
